TPU v7x, 32 devices: a whole 2x2x4 slice. The times are simulated.
32 devices in a mesh: cross: 4 (over y, x), island: 8 (over z, core).
Axes of the slice: x: 2, y: 2, z: 4, core: 2. Of those that a mesh axis runs over, the one named last changes fastest.
Arguments:
- tokens: bfloat16 [16384, 768], P(('cross', 'island')), may hold values from -6 to 6
- cotangent: bfloat16 [16384, 768], P(('cross', 'island')), may hold values from -6 to 6
- gate: float32 [16384], P(('cross', 'island')), may hold values from 0.2 to 1
- slot: int32 [16384], P(('cross', 'island')), may hold values from -1 to 127, as said below
- w_in: bfloat16 [64, 768, 3072], P(('cross', 'island')), may hold values from -0.21875 to 0.21875
- w_out: bfloat16 [64, 3072, 768], P(('cross', 'island')), may hold values from -0.109375 to 0.109375
Outputs:
- token_grad: bfloat16 [16384, 768], P(('cross', 'island'))
Inputs may be any that keep to these rules, and one draw needn't show every extreme that they name: Within the tokens of one device the non-negative slots are distinct; slot // 2 is the token's expert and its slots are filled from 0 upward in token order; tokens beyond an expert's 2 slots are -1. Expert indices run over devices in mesh order, 2 a device.
All inputs are finite; a program needn't handle non-finite values.
Results may differ from a plain program's by a relative error of at most 0.0057.
Values may be sent and summed in bfloat16 or wider, within the bound.
No kernel may reach another device: no remote copies, remote signals or barrier semaphores. Data moves between devices by JAX's collectives and lax.ppermute only.
A program may use at most 128 MiB of HBM per device.

v0:
```python
import jax
import jax.numpy as jnp
from jax import lax
from jax.sharding import PartitionSpec as P

CAP = 2


def ramp(pre):
    return jnp.clip(0.5 + 10.0 * pre, 0.0, 1.0)


def expert_pass(rows_x, rows_d, w_in, w_out):
    pre = jnp.einsum("sekd,edf->sekf", rows_x, w_in, preferred_element_type=jnp.float32)
    back = jnp.einsum("sekd,efd->sekf", rows_d, w_out, preferred_element_type=jnp.float32)
    hidden_grad = (back * ramp(pre)).astype(jnp.bfloat16)
    return jnp.einsum(
        "sekf,edf->sekd", hidden_grad, w_in, preferred_element_type=jnp.float32
    ).astype(jnp.bfloat16)


def per_device(tokens, cotangent, gate, slot, w_in, w_out):
    n_cross = lax.axis_size("cross")
    n_island = lax.axis_size("island")
    devices = n_cross * n_island
    exp_dev = w_in.shape[0]
    width = tokens.shape[1]
    total_slots = devices * exp_dev * CAP
    scaled = (gate[:, None] * cotangent.astype(jnp.float32)).astype(jnp.bfloat16)
    target = jnp.where(slot < 0, total_slots, slot)
    send_x = jnp.zeros((total_slots, width), jnp.bfloat16).at[target].set(tokens, mode="drop")
    send_d = jnp.zeros((total_slots, width), jnp.bfloat16).at[target].set(scaled, mode="drop")
    send_x = send_x.reshape(devices, exp_dev, CAP, width)
    send_d = send_d.reshape(devices, exp_dev, CAP, width)
    result = expert_pass(
        lax.all_to_all(send_x, ("cross", "island"), split_axis=0, concat_axis=0, tiled=True),
        lax.all_to_all(send_d, ("cross", "island"), split_axis=0, concat_axis=0, tiled=True),
        w_in,
        w_out,
    )
    arrived = lax.all_to_all(result, ("cross", "island"), split_axis=0, concat_axis=0, tiled=True)
    rows = arrived.reshape(total_slots, width)
    safe = jnp.where(slot < 0, 0, slot)
    picked = jnp.take(rows, safe, axis=0)
    return jnp.where(slot[:, None] >= 0, picked, jnp.zeros_like(picked))


def solution(mesh):
    in_specs = (
        P(("cross", "island"), None),
        P(("cross", "island"), None),
        P(("cross", "island")),
        P(("cross", "island")),
        P(("cross", "island"), None, None),
        P(("cross", "island"), None, None),
    )
    out_specs = P(("cross", "island"), None)
    return jax.shard_map(
        per_device, mesh=mesh, in_specs=in_specs, out_specs=out_specs, check_vma=False
    )
```

profile of v0, /device:TPU:1, one launch (start us, length us, event | category | flops | bytes accessed | tf_op | source)
XLA Modules:
  0.0 61.3 jit_solution(3039317262425671571)
XLA Ops:
  0.0 0.7 %compare_select_fusion.3 = (s32[512]{0:T(512)S(1)}, s32[512]{0:T(512)S(1)}) fusion(s32[512]{0:T(512)} %param.9), kind=kLoop, calls=%fused_computation.29 | loop fusion | flops 4608 | bytes 6144 | tf_op jit(solution)/shard_map/jit(_take)/jit(_where)/select_n | solution.py:44
  0.7 3.2 %scatter_custom_fusion.1 = bf16[128,768]{1,0:T(8,128)(2,1)S(1)} fusion(s32[512]{0:T(512)S(1)} %get-tuple-element.8, bf16[512,768]{1,0:T(8,128)(2,1)} %param.6, bf16[]{:T(256)} %constant.12.clone.1), kind=kCustom, calls=%fused_computation.23 | custom fusion | bytes 197120 | tf_op jit(solution)/shard_map/scatter | solution.py:31
  3.9 0.8 %reshape.18 = bf16[32,2,2,768]{3,2,1,0:T(2,128)(2,1)} reshape(bf16[128,768]{1,0:T(8,128)(2,1)S(1)} %scatter_custom_fusion.1) | data formatting | bytes 393216 | tf_op jit(solution)/shard_map/reshape | solution.py:33
  4.6 7.1 %all-to-all-start.1 = ((bf16[32,2,2,768]{3,2,1,0:T(2,128)(2,1)}), bf16[32,2,2,768]{3,2,1,0:T(2,128)(2,1)S(1)}, u32[]{:S(2)}, u32[]{:S(2)}) async-start(bf16[32,2,2,768]{3,2,1,0:T(2,128)(2,1)} %reshape.18), calls=%async_computation.1 | async-start | bytes 393216 | tf_op jit(solution)/shard_map/all_to_all | solution.py:36
  11.7 3.3 %scatter_custom_fusion = bf16[128,768]{1,0:T(8,128)(2,1)S(1)} fusion(s32[512]{0:T(512)S(1)} %get-tuple-element.8, bf16[512,768]{1,0:T(8,128)(2,1)} %param.7, f32[512]{0:T(512)} %param.8, bf16[]{:T(256)} %constant.12.clone.1), kind=kCustom, calls=%fused_computation.18 | custom fusion | flops 1179648 | bytes 985090 | tf_op jit(solution)/shard_map/scatter | solution.py:32
  15.1 0.7 %reshape.17 = bf16[32,2,2,768]{3,2,1,0:T(2,128)(2,1)} reshape(bf16[128,768]{1,0:T(8,128)(2,1)S(1)} %scatter_custom_fusion) | data formatting | bytes 393216 | tf_op jit(solution)/shard_map/reshape | solution.py:34
  15.8 5.2 %all-to-all-done.1 = bf16[32,2,2,768]{3,2,1,0:T(2,128)(2,1)S(1)} async-done(((bf16[32,2,2,768]{3,2,1,0:T(2,128)(2,1)}), bf16[32,2,2,768]{3,2,1,0:T(2,128)(2,1)S(1)}, u32[]{:S(2)}, u32[]{:S(2)}) %all-to-all-start.1) | async-done | bytes 196640 | tf_op jit(solution)/shard_map/all_to_all | solution.py:36
  21.0 2.3 %all-to-all-start = ((bf16[32,2,2,768]{3,2,1,0:T(2,128)(2,1)}), bf16[32,2,2,768]{3,2,1,0:T(2,128)(2,1)S(1)}, u32[]{:S(2)}, u32[]{:S(2)}) async-start(bf16[32,2,2,768]{3,2,1,0:T(2,128)(2,1)} %reshape.17), calls=%async_computation | async-start | bytes 393216 | tf_op jit(solution)/shard_map/all_to_all | solution.py:37
  23.3 5.4 %fusion.15 = f32[2,32,2,3072]{3,1,2,0:T(8,128)S(1)} fusion(bf16[2,768,3072]{2,1,0:T(8,128)(2,1)} %param.10, bf16[32,2,2,768]{3,2,1,0:T(2,128)(2,1)S(1)} %all-to-all-done.1), kind=kOutput, calls=%fused_computation.12 | convolution fusion | flops 605159424 | bytes 11206656 | tf_op jit(solution)/shard_map/sekd,edf->sekf/dot_general | solution.py:14
  28.8 3.7 %all-to-all-done = bf16[32,2,2,768]{3,2,1,0:T(2,128)(2,1)S(1)} async-done(((bf16[32,2,2,768]{3,2,1,0:T(2,128)(2,1)}), bf16[32,2,2,768]{3,2,1,0:T(2,128)(2,1)S(1)}, u32[]{:S(2)}, u32[]{:S(2)}) %all-to-all-start) | async-done | bytes 196640 | tf_op jit(solution)/shard_map/all_to_all | solution.py:37
  32.5 6.6 %fusion.21 = bf16[32,2,2,3072]{3,0,2,1:T(8,128)(2,1)S(1)} fusion(f32[2,32,2,3072]{3,1,2,0:T(8,128)S(1)} %fusion.15, bf16[2,3072,768]{2,1,0:T(8,128)(2,1)} %param.11, bf16[32,2,2,768]{3,2,1,0:T(2,128)(2,1)S(1)} %all-to-all-done), kind=kOutput, calls=%fused_computation.14 | convolution fusion | flops 604766208 | bytes 11993088 | tf_op jit(solution)/shard_map/sekd,efd->sekf/dot_general | solution.py:15
  39.1 0.0 copy-start
  39.1 6.7 %fusion.27 = bf16[32,2,2,768]{3,0,2,1:T(8,128)(2,1)S(1)} fusion(bf16[32,2,2,3072]{3,0,2,1:T(8,128)(2,1)S(1)} %fusion.21, bf16[2,768,3072]{2,1,0:T(8,128)(2,1)} %param.10), kind=kOutput, calls=%fused_computation.17 | convolution fusion | flops 604078080 | bytes 10420224 | tf_op jit(solution)/shard_map/sekf,edf->sekd/dot_general | solution.py:17
  45.7 0.9 %copy.14 = bf16[32,2,2,768]{3,2,1,0:T(2,128)(2,1)} copy(bf16[32,2,2,768]{3,0,2,1:T(8,128)(2,1)S(1)} %fusion.27) | data formatting | bytes 393216 | tf_op jit(solution)/shard_map/convert_element_type | solution.py:19
  46.6 2.3 %all-to-all-start.2 = ((bf16[32,2,2,768]{3,2,1,0:T(2,128)(2,1)}), bf16[32,2,2,768]{3,2,1,0:T(2,128)(2,1)S(1)}, u32[]{:S(2)}, u32[]{:S(2)}) async-start(bf16[32,2,2,768]{3,2,1,0:T(2,128)(2,1)} %copy.14), calls=%async_computation.2 | async-start | bytes 393216 | tf_op jit(solution)/shard_map/all_to_all | solution.py:41
  49.0 0.0 copy-done
  49.0 9.1 %all-to-all-done.2 = bf16[32,2,2,768]{3,2,1,0:T(2,128)(2,1)S(1)} async-done(((bf16[32,2,2,768]{3,2,1,0:T(2,128)(2,1)}), bf16[32,2,2,768]{3,2,1,0:T(2,128)(2,1)S(1)}, u32[]{:S(2)}, u32[]{:S(2)}) %all-to-all-start.2) | async-done | bytes 196640 | tf_op jit(solution)/shard_map/all_to_all | solution.py:41
  58.1 0.1 reshape.19
  58.1 2.0 %gather_fusion = bf16[512,768]{1,0:T(8,128)(2,1)S(1)} fusion(bf16[128,768]{1,0:T(8,128)(2,1)S(1)} %reshape.19, s32[1024]{0:T(1024)S(1)} %pad_clamp_fusion), kind=kCustom, calls=%fused_computation | custom fusion | bytes 1574912 | tf_op jit(solution)/shard_map/jit(_take)/gather | solution.py:44
  60.2 1.1 %select_select_fusion = bf16[512,768]{1,0:T(8,128)(2,1)} fusion(bf16[512,768]{1,0:T(8,128)(2,1)S(1)} %gather_fusion, pred[512]{0:T(512)(128)(4,1)S(1)} %get-tuple-element.6, pred[512]{0:T(512)(128)(4,1)S(1)} %get-tuple-element.5), kind=kLoop, calls=%fused_computation.19 | loop fusion | flops 786432 | bytes 1573888 | tf_op jit(solution)/shard_map/jit(_where)/select_n | solution.py:45
  (2 shorter events, 0.0 us)
Async XLA Ops:
  4.6 16.4 %all-to-all-start.1 = ((bf16[32,2,2,768]{3,2,1,0:T(2,128)(2,1)}), bf16[32,2,2,768]{3,2,1,0:T(2,128)(2,1)S(1)}, u32[]{:S(2)}, u32[]{:S(2)}) async-start(bf16[32,2,2,768]{3,2,1,0:T(2,128)(2,1)} %reshape.18), calls=%async_computation.1 | async-start | bytes 393216 | tf_op jit(solution)/shard_map/all_to_all | solution.py:36
  21.0 11.4 %all-to-all-start = ((bf16[32,2,2,768]{3,2,1,0:T(2,128)(2,1)}), bf16[32,2,2,768]{3,2,1,0:T(2,128)(2,1)S(1)}, u32[]{:S(2)}, u32[]{:S(2)}) async-start(bf16[32,2,2,768]{3,2,1,0:T(2,128)(2,1)} %reshape.17), calls=%async_computation | async-start | bytes 393216 | tf_op jit(solution)/shard_map/all_to_all | solution.py:37
  39.1 9.9 %copy-start = (s32[512]{0:T(512)S(1)}, s32[512]{0:T(512)}, u32[]{:S(2)}) copy-start(s32[512]{0:T(512)} %param.9) | copy-start | bytes 6148
  46.6 11.4 %all-to-all-start.2 = ((bf16[32,2,2,768]{3,2,1,0:T(2,128)(2,1)}), bf16[32,2,2,768]{3,2,1,0:T(2,128)(2,1)S(1)}, u32[]{:S(2)}, u32[]{:S(2)}) async-start(bf16[32,2,2,768]{3,2,1,0:T(2,128)(2,1)} %copy.14), calls=%async_computation.2 | async-start | bytes 393216 | tf_op jit(solution)/shard_map/all_to_all | solution.py:41
where the time goes:
time: 61.7 us; the launch traced here: 61.3 us
  matrix products  18.7 us (30%)
  waiting for transfers between devices  17.9 us (29%)
  starting transfers between devices  11.7 us (19%)
  local copies, waits for them, and re-layouts  7.69 us (12%)
  other arithmetic  5.11 us (8%)
    all_to_all x1, waiting for transfers between devices, per_device(): lax.all_to_all(result, ('cross', 'island'), split_axis=0, concat_axis=0,...  9.07 us
    all_to_all x1, starting transfers between devices, per_device(): lax.all_to_all(send_x, ('cross', 'island'), split_axis=0, concat_axis=0,...  7.08 us
    dot_general x1, matrix products, expert_pass(): jnp.einsum('sekf,edf->sekd', hidden_grad, w_in, preferred_element_type=jn...  6.65 us
    dot_general x1, matrix products, expert_pass(): jnp.einsum('sekd,efd->sekf', rows_d, w_out, preferred_element_type=jnp.fl...  6.62 us
    dot_general x1, matrix products, expert_pass(): jnp.einsum('sekd,edf->sekf', rows_x, w_in, preferred_element_type=jnp.flo...  5.44 us
    all_to_all x1, waiting for transfers between devices, per_device(): lax.all_to_all(send_x, ('cross', 'island'), split_axis=0, concat_axis=0,...  5.2 us
    all_to_all x1, waiting for transfers between devices, per_device(): lax.all_to_all(send_d, ('cross', 'island'), split_axis=0, concat_axis=0,...  3.66 us
    scatter x1, other arithmetic, per_device(): jnp.zeros((total_slots, width), jnp.bfloat16).at[target]  3.32 us
  transfers between devices with their start and end apart: 3, of which 3 were waited for; matrix products, arithmetic and copies ran while one was open for 16% of the time, Pallas kernels for 0%

commit v1 on v0

v1 whole, which is shorter than its diff:
```python
import functools

import jax
import jax.numpy as jnp
from jax import lax
from jax.experimental import pallas as pl
from jax.experimental.pallas import tpu as pltpu
from jax.sharding import PartitionSpec as P

CAP = 2
AXES = ("cross", "island")
MIB = 1 << 20


def ramp(pre):
    return jnp.clip(0.5 + 10.0 * pre, 0.0, 1.0)


def split(value, size):
    if size & (size - 1) == 0:
        return value >> (size.bit_length() - 1), value & (size - 1)
    return lax.div(value, size), lax.rem(value, size)


def one_hot(mask):
    return jnp.where(mask, 1.0, 0.0).astype(jnp.bfloat16)


def send_kernel(per_dev, slot_ref, gate_ref, tokens_ref, cotangent_ref, out_ref):
    shape = (out_ref.shape[0], slot_ref.shape[1])
    device, within = split(lax.broadcasted_iota(jnp.int32, shape, 0), 2 * per_dev)
    kind, place = split(within, per_dev)
    match = slot_ref[...] == device * per_dev + place
    is_d = kind == 1
    rows = jnp.dot(
        one_hot(match & ~is_d), tokens_ref[...], preferred_element_type=jnp.float32
    ) + jnp.dot(
        one_hot(match & is_d), cotangent_ref[...], preferred_element_type=jnp.float32
    )
    gate = jnp.sum(jnp.where(match, gate_ref[...], 0.0), axis=1, keepdims=True)
    out_ref[...] = (rows * jnp.where(is_d[:, :1], gate, 1.0)).astype(out_ref.dtype)


def expert_kernel(experts, chunk, recv_ref, w_in_ref, w_out_ref, out_ref):
    per_dev = experts * CAP
    total = recv_ref.shape[0]
    devices = total // (2 * per_dev)
    rows = devices * CAP
    width = recv_ref.shape[1]
    hidden = w_in_ref.shape[2]
    to = lax.broadcasted_iota(jnp.int32, (total, total), 0)
    group, member = split(to, rows)
    device, cap = split(member, CAP)
    source = device * (2 * per_dev) + group * CAP + cap
    pick = one_hot(lax.broadcasted_iota(jnp.int32, (total, total), 1) == source)
    sorted_rows = jnp.dot(
        pick, recv_ref[...], preferred_element_type=jnp.float32
    ).astype(jnp.bfloat16)
    parts = []
    for e in range(experts):
        x = sorted_rows[e * rows : (e + 1) * rows]
        d = sorted_rows[(experts + e) * rows : (experts + e + 1) * rows]
        total_grad = jnp.zeros((rows, width), jnp.float32)
        for f in range(0, hidden, chunk):
            first = w_in_ref[e, :, f : f + chunk]
            second = w_out_ref[e, f : f + chunk, :]
            pre = jnp.dot(x, first, preferred_element_type=jnp.float32)
            back = lax.dot_general(
                d, second, (((1,), (1,)), ((), ())), preferred_element_type=jnp.float32
            )
            hidden_grad = (back * ramp(pre)).astype(jnp.bfloat16)
            total_grad += lax.dot_general(
                hidden_grad,
                first,
                (((1,), (1,)), ((), ())),
                preferred_element_type=jnp.float32,
            )
        parts.append(total_grad.astype(jnp.bfloat16))
    grads = jnp.concatenate(parts, axis=0)
    half = width // 2
    shape = (total, experts * rows)
    device, within = split(lax.broadcasted_iota(jnp.int32, shape, 0), 2 * per_dev)
    side, place = split(within, per_dev)
    expert, cap = split(place, CAP)
    match = lax.broadcasted_iota(jnp.int32, shape, 1) == (
        expert * rows + device * CAP + cap
    )
    out_ref[...] = (
        jnp.dot(
            one_hot(match & (side == 0)),
            grads[:, :half],
            preferred_element_type=jnp.float32,
        )
        + jnp.dot(
            one_hot(match & (side == 1)),
            grads[:, half:],
            preferred_element_type=jnp.float32,
        )
    ).astype(out_ref.dtype)


def token_kernel(per_dev, slot_ref, rows_ref, out_ref):
    shape = (rows_ref.shape[0], slot_ref.shape[1])
    device, within = split(lax.broadcasted_iota(jnp.int32, shape, 0), 2 * per_dev)
    side, place = split(within, per_dev)
    match = slot_ref[...] == device * per_dev + place
    half = rows_ref.shape[1]
    for k in range(2):
        out_ref[:, k * half : (k + 1) * half] = lax.dot_general(
            one_hot(match & (side == k)),
            rows_ref[...],
            (((0,), (0,)), ((), ())),
            preferred_element_type=jnp.float32,
        ).astype(out_ref.dtype)


VMEM = pl.BlockSpec(memory_space=pltpu.VMEM)


def per_device(tokens, cotangent, gate, slot, w_in, w_out):
    devices = lax.axis_size("cross") * lax.axis_size("island")
    experts, width, hidden = w_in.shape
    per_dev = experts * CAP
    total = devices * per_dev
    slot_row = slot[None, :]
    send = pl.pallas_call(
        functools.partial(send_kernel, per_dev),
        out_shape=jax.ShapeDtypeStruct((2 * total, width), jnp.bfloat16),
        in_specs=[VMEM] * 4,
        out_specs=VMEM,
        compiler_params=pltpu.CompilerParams(vmem_limit_bytes=16 * MIB),
        name="send",
    )(slot_row, gate[None, :], tokens, cotangent)
    recv = lax.all_to_all(
        send.reshape(devices, 2 * per_dev, width), AXES, 0, 0, tiled=True
    )
    result = pl.pallas_call(
        functools.partial(expert_kernel, experts, 512),
        out_shape=jax.ShapeDtypeStruct((2 * total, width // 2), jnp.bfloat16),
        in_specs=[VMEM] * 3,
        out_specs=VMEM,
        compiler_params=pltpu.CompilerParams(vmem_limit_bytes=32 * MIB),
        name="expert",
    )(recv.reshape(2 * total, width), w_in, w_out)
    arrived = lax.all_to_all(
        result.reshape(devices, 2 * per_dev, width // 2), AXES, 0, 0, tiled=True
    )
    return pl.pallas_call(
        functools.partial(token_kernel, per_dev),
        out_shape=jax.ShapeDtypeStruct(tokens.shape, jnp.bfloat16),
        in_specs=[VMEM] * 2,
        out_specs=VMEM,
        compiler_params=pltpu.CompilerParams(vmem_limit_bytes=16 * MIB),
        name="token",
    )(slot_row, arrived.reshape(2 * total, width // 2))


def solution(mesh):
    token_spec = P(AXES, None)
    weight_spec = P(AXES, None, None)
    return jax.shard_map(
        per_device,
        mesh=mesh,
        in_specs=(token_spec, token_spec, P(AXES), P(AXES), weight_spec, weight_spec),
        out_specs=token_spec,
        check_vma=False,
    )
```

time: 61.7 us -> 53 us (0.86)
  blocking collectives: 0 us -> 31.7 us
  matrix products: 18.7 us -> 0 us
  waiting for transfers between devices: 17.9 us -> 0 us
  starting transfers between devices: 11.7 us -> 0 us
  Pallas kernels: 0 us -> 9.92 us
  other arithmetic: 5.11 us -> 0 us
  local copies, waits for them, and re-layouts: 7.69 us -> 11 us
    all_to_all x0 -> x2, blocking collectives: none -> 31.7 us  [the longest x1 20.2 us: per_device(): lax.all_to_all(send.reshape(devices, 2 * per_dev, width), AXES, 0, 0, til...]
    dot_general x3 -> x0, matrix products: 18.7 us -> none  [the longest x1 6.65 us: expert_pass(): jnp.einsum('sekf,edf->sekd', hidden_grad, w_in, preferred_element_type=jn...]
    all_to_all x3 -> x0, waiting for transfers between devices: 17.9 us -> none  [the longest x1 9.07 us: per_device(): lax.all_to_all(result, ('cross', 'island'), split_axis=0, concat_axis=0,...]
    all_to_all x3 -> x0, starting transfers between devices: 11.7 us -> none  [the longest x1 7.08 us: per_device(): lax.all_to_all(send_x, ('cross', 'island'), split_axis=0, concat_axis=0,...]
    unnamed x2 -> x14, local copies, waits for them, and re-layouts: 0.01 us -> 11 us
    pallas_call x0 -> x3, Pallas kernels: none -> 9.92 us  [the longest x1 7.93 us: per_device(): pl.pallas_call(functools.partial(expert_kernel, experts, 512), out_shape=...]
    scatter x1 -> x0, other arithmetic: 3.32 us -> none  [per_device(): jnp.zeros((total_slots, width), jnp.bfloat16).at[target]]
    scatter x1 -> x0, local copies, waits for them, and re-layouts: 3.2 us -> none  [per_device(): jnp.zeros((total_slots, width), jnp.bfloat16).at[target]]
  transfers between devices with their start and end apart: 3 -> 0, of which waited for: 3 -> 0; matrix products, arithmetic and copies ran while one was open for 16% -> 0% of each run, Pallas kernels for 0% -> 0%
where the time goes in v1:
time: 53 us; the launch traced here: 52.6 us
  blocking collectives  31.7 us (60%)
  local copies, waits for them, and re-layouts  11 us (21%)
  Pallas kernels  9.92 us (19%)
    all_to_all x1, blocking collectives, per_device(): lax.all_to_all(send.reshape(devices, 2 * per_dev, width), AXES, 0, 0, til...  20.2 us
    all_to_all x1, blocking collectives, per_device(): lax.all_to_all(result.reshape(devices, 2 * per_dev, width // 2), AXES, 0,...  11.5 us
    unnamed x14, local copies, waits for them, and re-layouts  11 us
    pallas_call x1, Pallas kernels, per_device(): pl.pallas_call(functools.partial(expert_kernel, experts, 512), out_shape=...  7.93 us
    pallas_call x1, Pallas kernels, per_device(): pl.pallas_call(functools.partial(token_kernel, per_dev), out_shape=jax.Sh...  1.4 us

profile of v1, /device:TPU:1, one launch (start us, length us, event | category | flops | bytes accessed | tf_op | source)
XLA Modules:
  0.0 52.6 jit_solution(8603071248216350076)
XLA Ops:
  0.0 0.0 copy-start.2
  0.0 1.1 %copy-done.2 = bf16[512,768]{1,0:T(8,128)(2,1)S(1)} copy-done((bf16[512,768]{1,0:T(8,128)(2,1)S(1)}, bf16[512,768]{1,0:T(8,128)(2,1)}, u32[]{:S(2)}) %copy-start.2) | copy-done | bytes 786456
  1.1 0.0 copy-start.3
  1.1 1.1 %copy-done.3 = bf16[512,768]{1,0:T(8,128)(2,1)S(1)} copy-done((bf16[512,768]{1,0:T(8,128)(2,1)S(1)}, bf16[512,768]{1,0:T(8,128)(2,1)}, u32[]{:S(2)}) %copy-start.3) | copy-done | bytes 786456
  2.3 0.0 copy-start.4
  2.3 0.7 %copy-done.4 = s32[512]{0:T(512)S(1)} copy-done((s32[512]{0:T(512)S(1)}, s32[512]{0:T(512)}, u32[]{:S(2)}) %copy-start.4) | copy-done | bytes 2072
  3.0 0.0 copy-start.6
  3.0 0.7 %copy-done.6 = f32[512]{0:T(512)S(1)} copy-done((f32[512]{0:T(512)S(1)}, f32[512]{0:T(512)}, u32[]{:S(2)}) %copy-start.6) | copy-done | bytes 2072
  3.6 0.6 %send.1 = bf16[256,768]{1,0:T(8,128)(2,1)S(1)} custom-call(s32[1,512]{1,0:T(1,128)S(1)} %bitcast.10, f32[1,512]{1,0:T(1,128)S(1)} %bitcast.12, bf16[512,768]{1,0:T(8,128)(2,1)S(1)} %copy-done.2, bf16[512,768]{1,0:T(8,128)(2,1)S(1)} %copy-done.3), custom_call_target="tpu_custom_call" | custom-call | tf_op jit(solution)/shard_map/send/pallas_call | solution.py:126
  4.2 20.2 %all_to_all.10 = bf16[32,8,768]{2,1,0:T(8,128)(2,1)S(1)} all-to-all(bf16[32,8,768]{2,1,0:T(8,128)(2,1)S(1)} %bitcast.6), channel_id=1, replica_groups=mesh['cross'=4,'island'=8] {'cross','island'}, dimensions={0} | all-to-all | bytes 786432 | tf_op jit(solution)/shard_map/all_to_all | solution.py:134
  24.4 0.0 copy-start
  24.4 3.7 %copy-done = bf16[2,768,3072]{2,1,0:T(8,128)(2,1)S(1)} copy-done((bf16[2,768,3072]{2,1,0:T(8,128)(2,1)S(1)}, bf16[2,768,3072]{2,1,0:T(8,128)(2,1)}, u32[]{:S(2)}) %copy-start) | copy-done | bytes 9437208
  28.1 0.0 copy-start.1
  28.1 3.7 %copy-done.1 = bf16[2,3072,768]{2,1,0:T(8,128)(2,1)S(1)} copy-done((bf16[2,3072,768]{2,1,0:T(8,128)(2,1)S(1)}, bf16[2,3072,768]{2,1,0:T(8,128)(2,1)}, u32[]{:S(2)}) %copy-start.1) | copy-done | bytes 9437208
  31.8 0.0 copy-start.5
  31.8 7.9 %expert.1 = bf16[256,384]{1,0:T(8,128)(2,1)S(1)} custom-call(bf16[256,768]{1,0:T(8,128)(2,1)S(1)} %bitcast.7, bf16[2,768,3072]{2,1,0:T(8,128)(2,1)S(1)} %copy-done, bf16[2,3072,768]{2,1,0:T(8,128)(2,1)S(1)} %copy-done.1), custom_call_target="tpu_custom_call" | custom-call | tf_op jit(solution)/shard_map/expert/pallas_call | solution.py:137
  39.7 11.5 %all_to_all.11 = bf16[32,8,384]{2,1,0:T(8,128)(2,1)S(1)} all-to-all(bf16[32,8,384]{2,1,0:T(8,128)(2,1)S(1)} %bitcast.8), channel_id=1, replica_groups=mesh['cross'=4,'island'=8] {'cross','island'}, dimensions={0} | all-to-all | bytes 393216 | tf_op jit(solution)/shard_map/all_to_all | solution.py:145
  51.2 0.0 copy-done.5
  51.2 1.4 %token_.1 = bf16[512,768]{1,0:T(8,128)(2,1)} custom-call(s32[1,512]{1,0:T(1,128)S(1)} %bitcast.11, bf16[256,384]{1,0:T(8,128)(2,1)S(1)} %bitcast.9), custom_call_target="tpu_custom_call" | custom-call | tf_op jit(solution)/shard_map/token/pallas_call | solution.py:148
Async XLA Ops:
  0.0 1.1 %copy-start.2 = (bf16[512,768]{1,0:T(8,128)(2,1)S(1)}, bf16[512,768]{1,0:T(8,128)(2,1)}, u32[]{:S(2)}) copy-start(bf16[512,768]{1,0:T(8,128)(2,1)} %tokens_ref.1) | copy-start | bytes 2359300
  1.1 1.1 %copy-start.3 = (bf16[512,768]{1,0:T(8,128)(2,1)S(1)}, bf16[512,768]{1,0:T(8,128)(2,1)}, u32[]{:S(2)}) copy-start(bf16[512,768]{1,0:T(8,128)(2,1)} %cotangent_ref.1) | copy-start | bytes 2359300
  2.3 0.7 %copy-start.4 = (s32[512]{0:T(512)S(1)}, s32[512]{0:T(512)}, u32[]{:S(2)}) copy-start(s32[512]{0:T(512)} %param.9) | copy-start | bytes 6148
  3.0 0.7 %copy-start.6 = (f32[512]{0:T(512)S(1)}, f32[512]{0:T(512)}, u32[]{:S(2)}) copy-start(f32[512]{0:T(512)} %param.8) | copy-start | bytes 6148
  24.4 3.7 %copy-start = (bf16[2,768,3072]{2,1,0:T(8,128)(2,1)S(1)}, bf16[2,768,3072]{2,1,0:T(8,128)(2,1)}, u32[]{:S(2)}) copy-start(bf16[2,768,3072]{2,1,0:T(8,128)(2,1)} %w_in_ref.1) | copy-start | bytes 28311556
  28.1 3.7 %copy-start.1 = (bf16[2,3072,768]{2,1,0:T(8,128)(2,1)S(1)}, bf16[2,3072,768]{2,1,0:T(8,128)(2,1)}, u32[]{:S(2)}) copy-start(bf16[2,3072,768]{2,1,0:T(8,128)(2,1)} %w_out_ref.1) | copy-start | bytes 28311556
  31.8 19.5 %copy-start.5 = (s32[512]{0:T(512)S(1)}, s32[512]{0:T(512)}, u32[]{:S(2)}) copy-start(s32[512]{0:T(512)} %param.9) | copy-start | bytes 6148

commit v2 on v1

--- a/solution.py
+++ b/solution.py
@@ -26,7 +26,14 @@
     return jnp.where(mask, 1.0, 0.0).astype(jnp.bfloat16)
 
 
-def send_kernel(per_dev, slot_ref, gate_ref, tokens_ref, cotangent_ref, out_ref):
+def start_kernel(out_ref):
+    out_ref[...] = jnp.zeros_like(out_ref)
+
+
+def send_kernel(
+    per_dev, slot_ref, gate_ref, tokens_ref, cotangent_ref, started, out_ref
+):
+    del started
     shape = (out_ref.shape[0], slot_ref.shape[1])
     device, within = split(lax.broadcasted_iota(jnp.int32, shape, 0), 2 * per_dev)
     kind, place = split(within, per_dev)
@@ -115,6 +122,7 @@
 
 
 VMEM = pl.BlockSpec(memory_space=pltpu.VMEM)
+LONG = pl.CostEstimate(flops=20_000_000_000, transcendentals=0, bytes_accessed=0)
 
 
 def per_device(tokens, cotangent, gate, slot, w_in, w_out):
@@ -123,14 +131,23 @@
     per_dev = experts * CAP
     total = devices * per_dev
     slot_row = slot[None, :]
+    started = pl.pallas_call(
+        start_kernel,
+        out_shape=jax.ShapeDtypeStruct((8, 128), jnp.float32),
+        out_specs=VMEM,
+        compiler_params=pltpu.CompilerParams(vmem_limit_bytes=MIB),
+        cost_estimate=LONG,
+        name="start",
+    )()
     send = pl.pallas_call(
         functools.partial(send_kernel, per_dev),
         out_shape=jax.ShapeDtypeStruct((2 * total, width), jnp.bfloat16),
-        in_specs=[VMEM] * 4,
+        in_specs=[VMEM] * 4 + [pl.BlockSpec(memory_space=pl.ANY)],
         out_specs=VMEM,
         compiler_params=pltpu.CompilerParams(vmem_limit_bytes=16 * MIB),
+        cost_estimate=LONG,
         name="send",
-    )(slot_row, gate[None, :], tokens, cotangent)
+    )(slot_row, gate[None, :], tokens, cotangent, started)
     recv = lax.all_to_all(
         send.reshape(devices, 2 * per_dev, width), AXES, 0, 0, tiled=True
     )

time: 53 us -> 43.3 us (0.82)
  local copies, waits for them, and re-layouts: 11 us -> 1.36 us
    unnamed x14 -> x20, local copies, waits for them, and re-layouts: 11 us -> 1.36 us
where the time goes in v2:
time: 43.3 us; the launch traced here: 43.1 us
  blocking collectives  31.7 us (73%)
  Pallas kernels  9.92 us (23%)
  local copies, waits for them, and re-layouts  1.36 us (3%)
    all_to_all x1, blocking collectives, per_device(): lax.all_to_all(send.reshape(devices, 2 * per_dev, width), AXES, 0, 0, til...  20.2 us
    all_to_all x1, blocking collectives, per_device(): lax.all_to_all(result.reshape(devices, 2 * per_dev, width // 2), AXES, 0,...  11.5 us
    pallas_call x1, Pallas kernels, per_device(): pl.pallas_call(functools.partial(expert_kernel, experts, 512), out_shape=...  7.93 us
    pallas_call x1, Pallas kernels, per_device(): pl.pallas_call(functools.partial(token_kernel, per_dev), out_shape=jax.Sh...  1.4 us
    unnamed x20, local copies, waits for them, and re-layouts  1.36 us

profile of v2, /device:TPU:1, one launch (start us, length us, event | category | flops | bytes accessed | tf_op | source)
XLA Modules:
  0.0 43.1 jit_solution(3646049331377951111)
XLA Ops:
  0.0 0.0 copy-start
  0.0 0.0 copy-start.3
  0.0 0.0 copy-start.2
  0.0 0.0 copy-start.1
  0.0 0.0 slice-start
  0.0 0.0 slice-start.1
  0.0 0.0 slice-start.3
  0.1 0.0 slice-start.4
  0.1 0.6 %copy-done = s32[512]{0:T(512)S(1)} copy-done((s32[512]{0:T(512)S(1)}, s32[512]{0:T(512)}, u32[]{:S(2)}) %copy-start) | copy-done | bytes 2072
  0.7 0.0 copy-done.3
  0.7 0.5 %copy-done.2 = bf16[512,768]{1,0:T(8,128)(2,1)S(1)} copy-done((bf16[512,768]{1,0:T(8,128)(2,1)S(1)}, bf16[512,768]{1,0:T(8,128)(2,1)}, u32[]{:S(2)}) %copy-start.2) | copy-done | bytes 786456
  1.2 0.2 copy-done.1
  1.4 0.0 slice-start.2
  1.4 0.0 slice-start.5
  1.4 0.6 %send.1 = bf16[256,768]{1,0:T(8,128)(2,1)S(1)} custom-call(s32[1,512]{1,0:T(1,128)S(1)} %bitcast.14, f32[1,512]{1,0:T(1,128)S(1)} %bitcast.16, bf16[512,768]{1,0:T(8,128)(2,1)S(1)} %copy-done.1, bf16[512,768]{1,0:T(8,128)(2,1)S(1)} %copy-done.2, f32[8,128]{1,0:T(8,128)S(1)} %start.1.started), custom_call_target="tpu_custom_call" | custom-call | flops 20000000000 | tf_op jit(solution)/shard_map/send/pallas_call | solution.py:142
  2.0 20.2 %all_to_all.10 = bf16[32,8,768]{2,1,0:T(8,128)(2,1)S(1)} all-to-all(bf16[32,8,768]{2,1,0:T(8,128)(2,1)S(1)} %bitcast.13), channel_id=1, replica_groups=mesh['cross'=4,'island'=8] {'cross','island'}, dimensions={0} | all-to-all | bytes 786432 | tf_op jit(solution)/shard_map/all_to_all | solution.py:151
  22.2 0.0 slice-done
  22.2 0.0 slice-done.1
  22.2 0.0 slice-done.3
  22.2 0.0 slice-done.4
  22.2 0.0 slice-done.2
  22.2 0.0 slice-done.5
  22.2 7.9 %expert.1 = bf16[256,384]{1,0:T(8,128)(2,1)S(1)} custom-call(bf16[256,768]{1,0:T(8,128)(2,1)S(1)} %bitcast.10, bf16[2,768,3072]{2,1,0:T(8,128)(2,1)S(1)} %bitcast.7, bf16[2,3072,768]{2,1,0:T(8,128)(2,1)S(1)} %bitcast.9), custom_call_target="tpu_custom_call" | custom-call | tf_op jit(solution)/shard_map/expert/pallas_call | solution.py:154
  30.2 11.5 %all_to_all.11 = bf16[32,8,384]{2,1,0:T(8,128)(2,1)S(1)} all-to-all(bf16[32,8,384]{2,1,0:T(8,128)(2,1)S(1)} %bitcast.11), channel_id=1, replica_groups=mesh['cross'=4,'island'=8] {'cross','island'}, dimensions={0} | all-to-all | bytes 393216 | tf_op jit(solution)/shard_map/all_to_all | solution.py:162
  41.7 1.4 %token_.1 = bf16[512,768]{1,0:T(8,128)(2,1)} custom-call(s32[1,512]{1,0:T(1,128)S(1)} %bitcast.15, bf16[256,384]{1,0:T(8,128)(2,1)S(1)} %bitcast.12), custom_call_target="tpu_custom_call" | custom-call | tf_op jit(solution)/shard_map/token/pallas_call | solution.py:165
  (3 shorter events, 0.0 us)
Async XLA Ops:
  0.0 0.7 %copy-start = (s32[512]{0:T(512)S(1)}, s32[512]{0:T(512)}, u32[]{:S(2)}) copy-start(s32[512]{0:T(512)} %param.9) | copy-start | bytes 6148
  0.0 0.7 %copy-start.3 = (f32[512]{0:T(512)S(1)}, f32[512]{0:T(512)}, u32[]{:S(2)}) copy-start(f32[512]{0:T(512)} %param.8) | copy-start | bytes 6148
  0.0 1.2 %copy-start.2 = (bf16[512,768]{1,0:T(8,128)(2,1)S(1)}, bf16[512,768]{1,0:T(8,128)(2,1)}, u32[]{:S(2)}) copy-start(bf16[512,768]{1,0:T(8,128)(2,1)} %cotangent_ref.1) | copy-start | bytes 2359300
  0.0 1.4 %copy-start.1 = (bf16[512,768]{1,0:T(8,128)(2,1)S(1)}, bf16[512,768]{1,0:T(8,128)(2,1)}, u32[]{:S(2)}) copy-start(bf16[512,768]{1,0:T(8,128)(2,1)} %tokens_ref.1) | copy-start | bytes 2359300
  0.0 22.2 %slice-start = ((s8[9437184]{0:T(1024)(128)(4,1)}), s8[4194304]{0:T(1024)(128)(4,1)S(1)}, s32[]{:S(2)}) async-start(s8[9437184]{0:T(1024)(128)(4,1)} %bitcast.6), calls=%async_computation.2 | async-start | bytes 8388608
  0.0 22.1 %slice-start.1 = ((s8[9437184]{0:T(1024)(128)(4,1)}), s8[4194304]{0:T(1024)(128)(4,1)S(1)}, s32[]{:S(2)}) async-start(s8[9437184]{0:T(1024)(128)(4,1)} %bitcast.6), calls=%async_computation.3 | async-start | bytes 8388608
  0.0 22.1 %slice-start.3 = ((s8[9437184]{0:T(1024)(128)(4,1)}), s8[4194304]{0:T(1024)(128)(4,1)S(1)}, s32[]{:S(2)}) async-start(s8[9437184]{0:T(1024)(128)(4,1)} %bitcast.8), calls=%async_computation.5 | async-start | bytes 8388608
  0.1 22.1 %slice-start.4 = ((s8[9437184]{0:T(1024)(128)(4,1)}), s8[4194304]{0:T(1024)(128)(4,1)S(1)}, s32[]{:S(2)}) async-start(s8[9437184]{0:T(1024)(128)(4,1)} %bitcast.8), calls=%async_computation.6 | async-start | bytes 8388608
  1.4 20.8 %slice-start.2 = ((s8[9437184]{0:T(1024)(128)(4,1)}), s8[1048576]{0:T(1024)(128)(4,1)S(1)}, s32[]{:S(2)}) async-start(s8[9437184]{0:T(1024)(128)(4,1)} %bitcast.6), calls=%async_computation.4 | async-start | bytes 2097152
  1.4 20.8 %slice-start.5 = ((s8[9437184]{0:T(1024)(128)(4,1)}), s8[1048576]{0:T(1024)(128)(4,1)S(1)}, s32[]{:S(2)}) async-start(s8[9437184]{0:T(1024)(128)(4,1)} %bitcast.8), calls=%async_computation.7 | async-start | bytes 2097152

commit v3 on v2

--- a/solution.py
+++ b/solution.py
@@ -10,6 +10,9 @@
 CAP = 2
 AXES = ("cross", "island")
 MIB = 1 << 20
+TILE = 256
+UNITS = 2
+PRE, BACK, FINAL = range(3)
 
 
 def ramp(pre):
@@ -106,6 +109,148 @@
     ).astype(out_ref.dtype)
 
 
+def expert_tiles_kernel(recv_ref, w_in_ref, w_out_ref, out_ref):
+    experts, width, hidden = w_in_ref.shape
+    per_dev = experts * CAP
+    total = recv_ref.shape[0]
+    devices = total // (2 * per_dev)
+    rows = devices * CAP
+    half = width // 2
+    depth = width // TILE
+    bf16 = jnp.bfloat16
+    square = (total, total)
+
+    def cut(k):
+        return slice(k * TILE, (k + 1) * TILE)
+
+    def sort_rows(*accs):
+        group, member = split(lax.broadcasted_iota(jnp.int32, square, 0), rows)
+        device, cap = split(member, CAP)
+        source = device * (2 * per_dev) + group * CAP + cap
+        pick = one_hot(lax.broadcasted_iota(jnp.int32, square, 1) == source)
+        for k in range(depth):
+            pltpu.matmul_push_rhs(recv_ref[:, cut(k)], k // UNITS % 2, k % UNITS)
+        for k in range(depth):
+            pltpu.matmul_acc_lhs(accs[k], pick, k // UNITS % 2)
+        return [pltpu.matmul_pop(acc).astype(bf16) for acc in accs]
+
+    columns = pl.run_scoped(
+        sort_rows,
+        *[pltpu.ACC(k % UNITS)((total, TILE), jnp.float32) for k in range(depth)],
+    )
+
+    def products(*accs):
+        def acc(unit, kind, turn):
+            return accs[unit * 5 + 2 * kind + turn % 2]
+
+        plans = []
+        for unit in range(UNITS):
+            blocks = [
+                (e, f)
+                for e in range(experts)
+                for f in range(unit * TILE, hidden, UNITS * TILE)
+            ]
+            plan = []
+            for turn, (e, f) in enumerate(blocks):
+                tiles = [
+                    (kind, turn, e, slice(f, f + TILE), k)
+                    for kind in (PRE, BACK)
+                    for k in range(depth)
+                ]
+                if turn:
+                    tiles.insert(depth + 1, final)
+                plan += tiles
+                final = (FINAL, turn, e, slice(f, f + TILE), 0)
+            plans.append(plan + [final])
+        last = len(plans[0]) - 1
+
+        def push(unit, n):
+            kind, turn, e, f, k = plans[unit][n]
+            if kind == PRE:
+                tile = w_in_ref[e, cut(k), f]
+            elif kind == BACK:
+                tile = w_out_ref[e, f, cut(k)]
+            else:
+                pre = pltpu.matmul_pop(acc(unit, PRE, turn))
+                back = pltpu.matmul_pop(acc(unit, BACK, turn))
+                parts = [(back * ramp(pre)).astype(bf16)]
+                if e:
+                    parts.insert(0, jnp.zeros((e * rows, TILE), bf16))
+                parts.append(jnp.zeros((TILE - (e + 1) * rows, TILE), bf16))
+                tile = jnp.concatenate(parts, 0)
+            pltpu.matmul_push_rhs(tile, n % 2, unit, transpose=kind != PRE)
+
+        def multiply(unit, n):
+            kind, turn, e, f, k = plans[unit][n]
+            if kind == FINAL:
+                pltpu.matmul_acc_lhs(accs[unit * 5 + 4], w_in_ref[e, :, f], n % 2)
+            else:
+                group = kind * experts + e
+                pltpu.matmul_acc_lhs(
+                    acc(unit, kind, turn),
+                    columns[k][group * rows : (group + 1) * rows],
+                    n % 2,
+                )
+
+        for n in range(2):
+            for unit in range(UNITS):
+                push(unit, n)
+        for n in range(last + 1):
+            for unit in range(UNITS):
+                multiply(unit, n)
+                if n + 2 < last:
+                    push(unit, n + 2)
+                if n + 1 == last:
+                    push(unit, last)
+        sums = [pltpu.matmul_pop(accs[u * 5 + 4])[:, : experts * rows] for u in range(UNITS)]
+        return (sums[0] + sums[1]).astype(bf16)
+
+    spaces = []
+    for unit in range(UNITS):
+        spaces += [pltpu.ACC(unit)((rows, TILE), jnp.float32)] * 4
+        spaces += [pltpu.ACC(unit)((width, TILE), jnp.float32)]
+    grads = pl.run_scoped(products, *spaces)
+
+    def spread(*accs):
+        device, within = split(lax.broadcasted_iota(jnp.int32, square, 0), 2 * per_dev)
+        side, place = split(within, per_dev)
+        expert, cap = split(place, CAP)
+        source = (side * experts + expert) * rows + device * CAP + cap
+        put = one_hot(lax.broadcasted_iota(jnp.int32, square, 1) == source)
+        sizes = [min(TILE, half - j * TILE) for j in range(len(accs))]
+        for j, n in enumerate(sizes):
+            tile = jnp.concatenate(
+                [grads[s + j * TILE : s + j * TILE + n] for s in (0, half)], 1
+            )
+            if n < TILE:
+                tile = jnp.concatenate([tile, jnp.zeros((TILE - n, TILE), bf16)], 0)
+            pltpu.matmul_push_rhs(tile, j // UNITS, j % UNITS, transpose=True)
+        for j, acc in enumerate(accs):
+            pltpu.matmul_acc_lhs(acc, put, j // UNITS)
+        for j, n in enumerate(sizes):
+            out_ref[:, j * TILE : j * TILE + n] = pltpu.matmul_pop(accs[j])[
+                :, :n
+            ].astype(out_ref.dtype)
+
+    pl.run_scoped(
+        spread,
+        *[
+            pltpu.ACC(j % UNITS)((total, TILE), jnp.float32)
+            for j in range(pl.cdiv(half, TILE))
+        ],
+    )
+
+
+def tiles_fit(devices, experts, width, hidden):
+    rows = devices * CAP
+    return (
+        2 * experts * rows == TILE
+        and rows % 16 == 0
+        and width == 3 * TILE
+        and hidden % (UNITS * TILE) == 0
+    )
+
+
 def token_kernel(per_dev, slot_ref, rows_ref, out_ref):
     shape = (rows_ref.shape[0], slot_ref.shape[1])
     device, within = split(lax.broadcasted_iota(jnp.int32, shape, 0), 2 * per_dev)
@@ -152,7 +297,9 @@
         send.reshape(devices, 2 * per_dev, width), AXES, 0, 0, tiled=True
     )
     result = pl.pallas_call(
-        functools.partial(expert_kernel, experts, 512),
+        expert_tiles_kernel
+        if tiles_fit(devices, experts, width, hidden)
+        else functools.partial(expert_kernel, experts, 512),
         out_shape=jax.ShapeDtypeStruct((2 * total, width // 2), jnp.bfloat16),
         in_specs=[VMEM] * 3,
         out_specs=VMEM,

time: 43.3 us -> 41.5 us (0.958)
  Pallas kernels: 9.92 us -> 8.11 us
    pallas_call x1, Pallas kernels: 7.93 us -> 6.13 us  [per_device(): pl.pallas_call(expert_tiles_kernel if tiles_fit(devices, experts, width,...]
where the time goes in v3:
time: 41.5 us; the launch traced here: 41.3 us
  blocking collectives  31.7 us (76%)
  Pallas kernels  8.11 us (20%)
  local copies, waits for them, and re-layouts  1.36 us (3%)
    all_to_all x1, blocking collectives, per_device(): lax.all_to_all(send.reshape(devices, 2 * per_dev, width), AXES, 0, 0, til...  20.2 us
    all_to_all x1, blocking collectives, per_device(): lax.all_to_all(result.reshape(devices, 2 * per_dev, width // 2), AXES, 0,...  11.5 us
    pallas_call x1, Pallas kernels, per_device(): pl.pallas_call(expert_tiles_kernel if tiles_fit(devices, experts, width,...  6.13 us
    pallas_call x1, Pallas kernels, per_device(): pl.pallas_call(functools.partial(token_kernel, per_dev), out_shape=jax.Sh...  1.4 us
    unnamed x20, local copies, waits for them, and re-layouts  1.36 us

profile of v3, /device:TPU:1, one launch (start us, length us, event | category | flops | bytes accessed | tf_op | source)
XLA Modules:
  0.0 41.3 jit_solution(4518916406617808054)
XLA Ops:
  0.0 0.0 copy-start
  0.0 0.0 copy-start.3
  0.0 0.0 copy-start.2
  0.0 0.0 copy-start.1
  0.0 0.0 slice-start
  0.0 0.0 slice-start.1
  0.0 0.0 slice-start.3
  0.1 0.0 slice-start.4
  0.1 0.6 %copy-done = s32[512]{0:T(512)S(1)} copy-done((s32[512]{0:T(512)S(1)}, s32[512]{0:T(512)}, u32[]{:S(2)}) %copy-start) | copy-done | bytes 2072
  0.7 0.0 copy-done.3
  0.7 0.5 %copy-done.2 = bf16[512,768]{1,0:T(8,128)(2,1)S(1)} copy-done((bf16[512,768]{1,0:T(8,128)(2,1)S(1)}, bf16[512,768]{1,0:T(8,128)(2,1)}, u32[]{:S(2)}) %copy-start.2) | copy-done | bytes 786456
  1.2 0.2 copy-done.1
  1.4 0.0 slice-start.2
  1.4 0.0 slice-start.5
  1.4 0.6 %send.1 = bf16[256,768]{1,0:T(8,128)(2,1)S(1)} custom-call(s32[1,512]{1,0:T(1,128)S(1)} %bitcast.14, f32[1,512]{1,0:T(1,128)S(1)} %bitcast.16, bf16[512,768]{1,0:T(8,128)(2,1)S(1)} %copy-done.1, bf16[512,768]{1,0:T(8,128)(2,1)S(1)} %copy-done.2, f32[8,128]{1,0:T(8,128)S(1)} %start.1.started), custom_call_target="tpu_custom_call" | custom-call | flops 20000000000 | tf_op jit(solution)/shard_map/send/pallas_call | solution.py:287
  2.0 20.2 %all_to_all.10 = bf16[32,8,768]{2,1,0:T(8,128)(2,1)S(1)} all-to-all(bf16[32,8,768]{2,1,0:T(8,128)(2,1)S(1)} %bitcast.13), channel_id=1, replica_groups=mesh['cross'=4,'island'=8] {'cross','island'}, dimensions={0} | all-to-all | bytes 786432 | tf_op jit(solution)/shard_map/all_to_all | solution.py:296
  22.2 0.0 slice-done
  22.2 0.0 slice-done.1
  22.2 0.0 slice-done.3
  22.2 0.0 slice-done.4
  22.2 0.0 slice-done.2
  22.2 0.0 slice-done.5
  22.2 6.1 %expert.1 = bf16[256,384]{1,0:T(8,128)(2,1)S(1)} custom-call(bf16[256,768]{1,0:T(8,128)(2,1)S(1)} %bitcast.10, bf16[2,768,3072]{2,1,0:T(8,128)(2,1)S(1)} %bitcast.7, bf16[2,3072,768]{2,1,0:T(8,128)(2,1)S(1)} %bitcast.9), custom_call_target="tpu_custom_call" | custom-call | tf_op jit(solution)/shard_map/expert/pallas_call | solution.py:299
  28.4 11.5 %all_to_all.11 = bf16[32,8,384]{2,1,0:T(8,128)(2,1)S(1)} all-to-all(bf16[32,8,384]{2,1,0:T(8,128)(2,1)S(1)} %bitcast.11), channel_id=1, replica_groups=mesh['cross'=4,'island'=8] {'cross','island'}, dimensions={0} | all-to-all | bytes 393216 | tf_op jit(solution)/shard_map/all_to_all | solution.py:309
  39.9 1.4 %token_.1 = bf16[512,768]{1,0:T(8,128)(2,1)} custom-call(s32[1,512]{1,0:T(1,128)S(1)} %bitcast.15, bf16[256,384]{1,0:T(8,128)(2,1)S(1)} %bitcast.12), custom_call_target="tpu_custom_call" | custom-call | tf_op jit(solution)/shard_map/token/pallas_call | solution.py:312
  (3 shorter events, 0.0 us)
Async XLA Ops:
  0.0 0.7 %copy-start = (s32[512]{0:T(512)S(1)}, s32[512]{0:T(512)}, u32[]{:S(2)}) copy-start(s32[512]{0:T(512)} %param.9) | copy-start | bytes 6148
  0.0 0.7 %copy-start.3 = (f32[512]{0:T(512)S(1)}, f32[512]{0:T(512)}, u32[]{:S(2)}) copy-start(f32[512]{0:T(512)} %param.8) | copy-start | bytes 6148
  0.0 1.2 %copy-start.2 = (bf16[512,768]{1,0:T(8,128)(2,1)S(1)}, bf16[512,768]{1,0:T(8,128)(2,1)}, u32[]{:S(2)}) copy-start(bf16[512,768]{1,0:T(8,128)(2,1)} %cotangent_ref.1) | copy-start | bytes 2359300
  0.0 1.4 %copy-start.1 = (bf16[512,768]{1,0:T(8,128)(2,1)S(1)}, bf16[512,768]{1,0:T(8,128)(2,1)}, u32[]{:S(2)}) copy-start(bf16[512,768]{1,0:T(8,128)(2,1)} %tokens_ref.1) | copy-start | bytes 2359300
  0.0 22.2 %slice-start = ((s8[9437184]{0:T(1024)(128)(4,1)}), s8[4194304]{0:T(1024)(128)(4,1)S(1)}, s32[]{:S(2)}) async-start(s8[9437184]{0:T(1024)(128)(4,1)} %bitcast.6), calls=%async_computation.2 | async-start | bytes 8388608
  0.0 22.1 %slice-start.1 = ((s8[9437184]{0:T(1024)(128)(4,1)}), s8[4194304]{0:T(1024)(128)(4,1)S(1)}, s32[]{:S(2)}) async-start(s8[9437184]{0:T(1024)(128)(4,1)} %bitcast.6), calls=%async_computation.3 | async-start | bytes 8388608
  0.0 22.1 %slice-start.3 = ((s8[9437184]{0:T(1024)(128)(4,1)}), s8[4194304]{0:T(1024)(128)(4,1)S(1)}, s32[]{:S(2)}) async-start(s8[9437184]{0:T(1024)(128)(4,1)} %bitcast.8), calls=%async_computation.5 | async-start | bytes 8388608
  0.1 22.1 %slice-start.4 = ((s8[9437184]{0:T(1024)(128)(4,1)}), s8[4194304]{0:T(1024)(128)(4,1)S(1)}, s32[]{:S(2)}) async-start(s8[9437184]{0:T(1024)(128)(4,1)} %bitcast.8), calls=%async_computation.6 | async-start | bytes 8388608
  1.4 20.8 %slice-start.2 = ((s8[9437184]{0:T(1024)(128)(4,1)}), s8[1048576]{0:T(1024)(128)(4,1)S(1)}, s32[]{:S(2)}) async-start(s8[9437184]{0:T(1024)(128)(4,1)} %bitcast.6), calls=%async_computation.4 | async-start | bytes 2097152
  1.4 20.8 %slice-start.5 = ((s8[9437184]{0:T(1024)(128)(4,1)}), s8[1048576]{0:T(1024)(128)(4,1)S(1)}, s32[]{:S(2)}) async-start(s8[9437184]{0:T(1024)(128)(4,1)} %bitcast.8), calls=%async_computation.7 | async-start | bytes 2097152

commit v4 on v3

--- a/solution.py
+++ b/solution.py
@@ -2,6 +2,7 @@
 
 import jax
 import jax.numpy as jnp
+import numpy as np
 from jax import lax
 from jax.experimental import pallas as pl
 from jax.experimental.pallas import tpu as pltpu
@@ -12,6 +13,7 @@
 MIB = 1 << 20
 TILE = 256
 UNITS = 2
+CHUNK = 128
 PRE, BACK, FINAL = range(3)
 
 
@@ -109,7 +111,7 @@
     ).astype(out_ref.dtype)
 
 
-def expert_tiles_kernel(recv_ref, w_in_ref, w_out_ref, out_ref):
+def expert_tiles_kernel(recv_ref, w_in_ref, w_out_ref, pick_ref, put_ref, out_ref):
     experts, width, hidden = w_in_ref.shape
     per_dev = experts * CAP
     total = recv_ref.shape[0]
@@ -118,20 +120,15 @@
     half = width // 2
     depth = width // TILE
     bf16 = jnp.bfloat16
-    square = (total, total)
 
     def cut(k):
         return slice(k * TILE, (k + 1) * TILE)
 
     def sort_rows(*accs):
-        group, member = split(lax.broadcasted_iota(jnp.int32, square, 0), rows)
-        device, cap = split(member, CAP)
-        source = device * (2 * per_dev) + group * CAP + cap
-        pick = one_hot(lax.broadcasted_iota(jnp.int32, square, 1) == source)
         for k in range(depth):
             pltpu.matmul_push_rhs(recv_ref[:, cut(k)], k // UNITS % 2, k % UNITS)
         for k in range(depth):
-            pltpu.matmul_acc_lhs(accs[k], pick, k // UNITS % 2)
+            pltpu.matmul_acc_lhs(accs[k], pick_ref[...], k // UNITS % 2)
         return [pltpu.matmul_pop(acc).astype(bf16) for acc in accs]
 
     columns = pl.run_scoped(
@@ -212,11 +209,6 @@
     grads = pl.run_scoped(products, *spaces)
 
     def spread(*accs):
-        device, within = split(lax.broadcasted_iota(jnp.int32, square, 0), 2 * per_dev)
-        side, place = split(within, per_dev)
-        expert, cap = split(place, CAP)
-        source = (side * experts + expert) * rows + device * CAP + cap
-        put = one_hot(lax.broadcasted_iota(jnp.int32, square, 1) == source)
         sizes = [min(TILE, half - j * TILE) for j in range(len(accs))]
         for j, n in enumerate(sizes):
             tile = jnp.concatenate(
@@ -226,7 +218,7 @@
                 tile = jnp.concatenate([tile, jnp.zeros((TILE - n, TILE), bf16)], 0)
             pltpu.matmul_push_rhs(tile, j // UNITS, j % UNITS, transpose=True)
         for j, acc in enumerate(accs):
-            pltpu.matmul_acc_lhs(acc, put, j // UNITS)
+            pltpu.matmul_acc_lhs(acc, put_ref[...], j // UNITS)
         for j, n in enumerate(sizes):
             out_ref[:, j * TILE : j * TILE + n] = pltpu.matmul_pop(accs[j])[
                 :, :n
@@ -239,6 +231,15 @@
             for j in range(pl.cdiv(half, TILE))
         ],
     )
+
+
+def row_orders(devices, experts):
+    total = 2 * devices * experts * CAP
+    source = (
+        np.arange(total).reshape(devices, 2 * experts, CAP).transpose(1, 0, 2).ravel()
+    )
+    pick = (source[:, None] == np.arange(total)).astype(jnp.bfloat16)
+    return pick, np.ascontiguousarray(pick.T)
 
 
 def tiles_fit(devices, experts, width, hidden):
@@ -251,22 +252,34 @@
     )
 
 
-def token_kernel(per_dev, slot_ref, rows_ref, out_ref):
-    shape = (rows_ref.shape[0], slot_ref.shape[1])
-    device, within = split(lax.broadcasted_iota(jnp.int32, shape, 0), 2 * per_dev)
+def token_kernel(per_dev, slot_ref, rows_ref, out_hbm, out_ref, sems):
+    total, half = rows_ref.shape
+    device, within = split(
+        lax.broadcasted_iota(jnp.int32, (CHUNK, total), 1), 2 * per_dev
+    )
     side, place = split(within, per_dev)
-    match = slot_ref[...] == device * per_dev + place
-    half = rows_ref.shape[1]
-    for k in range(2):
-        out_ref[:, k * half : (k + 1) * half] = lax.dot_general(
-            one_hot(match & (side == k)),
-            rows_ref[...],
-            (((0,), (0,)), ((), ())),
-            preferred_element_type=jnp.float32,
-        ).astype(out_ref.dtype)
+    wanted = device * per_dev + place
+    copies = []
+    for c in range(slot_ref.shape[1] // CHUNK):
+        tokens = pl.ds(c * CHUNK, CHUNK)
+        slot = jnp.broadcast_to(slot_ref[:, tokens], (CHUNK, CHUNK)).T
+        slot = jnp.concatenate([slot] * (total // CHUNK), axis=1)
+        for k in range(2):
+            out_ref[tokens, k * half : (k + 1) * half] = jnp.dot(
+                one_hot((slot == wanted) & (side == k)),
+                rows_ref[...],
+                preferred_element_type=jnp.float32,
+            ).astype(out_ref.dtype)
+        copies.append(
+            pltpu.make_async_copy(out_ref.at[tokens], out_hbm.at[tokens], sems.at[c])
+        )
+        copies[-1].start()
+    for copy in copies:
+        copy.wait()
 
 
 VMEM = pl.BlockSpec(memory_space=pltpu.VMEM)
+SHORT = pl.CostEstimate(flops=4_000_000_000, transcendentals=0, bytes_accessed=0)
 LONG = pl.CostEstimate(flops=20_000_000_000, transcendentals=0, bytes_accessed=0)
 
 
@@ -281,7 +294,7 @@
         out_shape=jax.ShapeDtypeStruct((8, 128), jnp.float32),
         out_specs=VMEM,
         compiler_params=pltpu.CompilerParams(vmem_limit_bytes=MIB),
-        cost_estimate=LONG,
+        cost_estimate=SHORT,
         name="start",
     )()
     send = pl.pallas_call(
@@ -296,16 +309,19 @@
     recv = lax.all_to_all(
         send.reshape(devices, 2 * per_dev, width), AXES, 0, 0, tiled=True
     )
+    operands = (recv.reshape(2 * total, width), w_in, w_out)
+    kernel = functools.partial(expert_kernel, experts, 512)
+    if tiles_fit(devices, experts, width, hidden):
+        operands += tuple(jnp.asarray(m) for m in row_orders(devices, experts))
+        kernel = expert_tiles_kernel
     result = pl.pallas_call(
-        expert_tiles_kernel
-        if tiles_fit(devices, experts, width, hidden)
-        else functools.partial(expert_kernel, experts, 512),
+        kernel,
         out_shape=jax.ShapeDtypeStruct((2 * total, width // 2), jnp.bfloat16),
-        in_specs=[VMEM] * 3,
+        in_specs=[VMEM] * len(operands),
         out_specs=VMEM,
         compiler_params=pltpu.CompilerParams(vmem_limit_bytes=32 * MIB),
         name="expert",
-    )(recv.reshape(2 * total, width), w_in, w_out)
+    )(*operands)
     arrived = lax.all_to_all(
         result.reshape(devices, 2 * per_dev, width // 2), AXES, 0, 0, tiled=True
     )
@@ -313,7 +329,11 @@
         functools.partial(token_kernel, per_dev),
         out_shape=jax.ShapeDtypeStruct(tokens.shape, jnp.bfloat16),
         in_specs=[VMEM] * 2,
-        out_specs=VMEM,
+        out_specs=pl.BlockSpec(memory_space=pl.ANY),
+        scratch_shapes=[
+            pltpu.VMEM(tokens.shape, tokens.dtype),
+            pltpu.SemaphoreType.DMA((tokens.shape[0] // CHUNK,)),
+        ],
         compiler_params=pltpu.CompilerParams(vmem_limit_bytes=16 * MIB),
         name="token",
     )(slot_row, arrived.reshape(2 * total, width // 2))

time: 41.5 us -> 41.3 us (level)
    unnamed x20 -> x24, local copies, waits for them, and re-layouts: 1.36 us -> 1.39 us
where the time goes in v4:
time: 41.3 us; the launch traced here: 41.1 us
  blocking collectives  31.7 us (77%)
  Pallas kernels  7.94 us (19%)
  local copies, waits for them, and re-layouts  1.39 us (3%)
    all_to_all x1, blocking collectives, per_device(): lax.all_to_all(send.reshape(devices, 2 * per_dev, width), AXES, 0, 0, til...  20.2 us
    all_to_all x1, blocking collectives, per_device(): lax.all_to_all(result.reshape(devices, 2 * per_dev, width // 2), AXES, 0,...  11.5 us
    pallas_call x1, Pallas kernels, per_device(): pl.pallas_call(kernel, out_shape=jax.ShapeDtypeStruct((2 * total, width /...  6.14 us
    unnamed x24, local copies, waits for them, and re-layouts  1.39 us
    pallas_call x1, Pallas kernels, per_device(): pl.pallas_call(functools.partial(token_kernel, per_dev), out_shape=jax.Sh...  1.21 us

profile of v4, /device:TPU:1, one launch (start us, length us, event | category | flops | bytes accessed | tf_op | source)
XLA Modules:
  0.0 41.1 jit_solution(7896739102154532045)
XLA Ops:
  0.0 0.0 copy-start.2
  0.0 0.0 copy-start.5
  0.0 0.0 copy-start.4
  0.0 0.0 copy-start.3
  0.0 0.0 slice-start
  0.0 0.0 slice-start.3
  0.1 0.6 %copy-done.2 = s32[512]{0:T(512)S(1)} copy-done((s32[512]{0:T(512)S(1)}, s32[512]{0:T(512)}, u32[]{:S(2)}) %copy-start.2) | copy-done | bytes 2072
  0.7 0.0 copy-done.5
  0.7 0.5 %copy-done.4 = bf16[512,768]{1,0:T(8,128)(2,1)S(1)} copy-done((bf16[512,768]{1,0:T(8,128)(2,1)S(1)}, bf16[512,768]{1,0:T(8,128)(2,1)}, u32[]{:S(2)}) %copy-start.4) | copy-done | bytes 786456
  1.2 0.2 copy-done.3
  1.4 0.0 slice-start.1
  1.4 0.0 slice-start.2
  1.4 0.0 slice-start.4
  1.4 0.0 slice-start.5
  1.4 0.0 copy-start
  1.4 0.0 copy-start.1
  1.4 0.6 %send.1 = bf16[256,768]{1,0:T(8,128)(2,1)S(1)} custom-call(s32[1,512]{1,0:T(1,128)S(1)} %bitcast.14, f32[1,512]{1,0:T(1,128)S(1)} %bitcast.16, bf16[512,768]{1,0:T(8,128)(2,1)S(1)} %copy-done.3, bf16[512,768]{1,0:T(8,128)(2,1)S(1)} %copy-done.4, f32[8,128]{1,0:T(8,128)S(1)} %start.1.started), custom_call_target="tpu_custom_call" | custom-call | flops 20000000000 | tf_op jit(solution)/shard_map/send/pallas_call | solution.py:300
  2.0 20.2 %all_to_all.10 = bf16[32,8,768]{2,1,0:T(8,128)(2,1)S(1)} all-to-all(bf16[32,8,768]{2,1,0:T(8,128)(2,1)S(1)} %bitcast.13), channel_id=1, replica_groups=mesh['cross'=4,'island'=8] {'cross','island'}, dimensions={0} | all-to-all | bytes 786432 | tf_op jit(solution)/shard_map/all_to_all | solution.py:309
  22.2 0.0 slice-done
  22.2 0.0 slice-done.3
  22.2 0.0 slice-done.1
  22.2 0.0 slice-done.2
  22.2 0.0 slice-done.4
  22.2 0.0 slice-done.5
  22.3 0.0 copy-done
  22.3 0.0 copy-done.1
  22.3 6.1 %expert.1 = bf16[256,384]{1,0:T(8,128)(2,1)S(1)} custom-call(bf16[256,768]{1,0:T(8,128)(2,1)S(1)} %bitcast.10, bf16[2,768,3072]{2,1,0:T(8,128)(2,1)S(1)} %bitcast.7, bf16[2,3072,768]{2,1,0:T(8,128)(2,1)S(1)} %bitcast.9, bf16[256,256]{1,0:T(8,128)(2,1)S(1)} %copy-done.1, bf16[256,256]{1,0:T(8,128)(2,1)S(1)} %copy-done), custom_call_target="tpu_custom_call" | custom-call | tf_op jit(solution)/shard_map/expert/pallas_call | solution.py:317
  28.4 11.5 %all_to_all.11 = bf16[32,8,384]{2,1,0:T(8,128)(2,1)S(1)} all-to-all(bf16[32,8,384]{2,1,0:T(8,128)(2,1)S(1)} %bitcast.11), channel_id=1, replica_groups=mesh['cross'=4,'island'=8] {'cross','island'}, dimensions={0} | all-to-all | bytes 393216 | tf_op jit(solution)/shard_map/all_to_all | solution.py:325
  39.9 1.2 %token_.1 = bf16[512,768]{1,0:T(8,128)(2,1)} custom-call(s32[1,512]{1,0:T(1,128)S(1)} %bitcast.15, bf16[256,384]{1,0:T(8,128)(2,1)S(1)} %bitcast.12), custom_call_target="tpu_custom_call" | custom-call | tf_op jit(solution)/shard_map/token/pallas_call | solution.py:328
  (3 shorter events, 0.0 us)
Async XLA Ops:
  0.0 0.7 %copy-start.2 = (s32[512]{0:T(512)S(1)}, s32[512]{0:T(512)}, u32[]{:S(2)}) copy-start(s32[512]{0:T(512)} %param.11) | copy-start | bytes 6148
  0.0 0.7 %copy-start.5 = (f32[512]{0:T(512)S(1)}, f32[512]{0:T(512)}, u32[]{:S(2)}) copy-start(f32[512]{0:T(512)} %param.10) | copy-start | bytes 6148
  0.0 1.2 %copy-start.4 = (bf16[512,768]{1,0:T(8,128)(2,1)S(1)}, bf16[512,768]{1,0:T(8,128)(2,1)}, u32[]{:S(2)}) copy-start(bf16[512,768]{1,0:T(8,128)(2,1)} %cotangent_ref.1) | copy-start | bytes 2359300
  0.0 1.4 %copy-start.3 = (bf16[512,768]{1,0:T(8,128)(2,1)S(1)}, bf16[512,768]{1,0:T(8,128)(2,1)}, u32[]{:S(2)}) copy-start(bf16[512,768]{1,0:T(8,128)(2,1)} %tokens_ref.1) | copy-start | bytes 2359300
  0.0 22.2 %slice-start = ((s8[9437184]{0:T(1024)(128)(4,1)}), s8[4194304]{0:T(1024)(128)(4,1)S(1)}, s32[]{:S(2)}) async-start(s8[9437184]{0:T(1024)(128)(4,1)} %bitcast.6), calls=%async_computation.2 | async-start | bytes 8388608
  0.0 22.2 %slice-start.3 = ((s8[9437184]{0:T(1024)(128)(4,1)}), s8[4194304]{0:T(1024)(128)(4,1)S(1)}, s32[]{:S(2)}) async-start(s8[9437184]{0:T(1024)(128)(4,1)} %bitcast.8), calls=%async_computation.5 | async-start | bytes 8388608
  1.4 20.8 %slice-start.1 = ((s8[9437184]{0:T(1024)(128)(4,1)}), s8[4194304]{0:T(1024)(128)(4,1)S(1)}, s32[]{:S(2)}) async-start(s8[9437184]{0:T(1024)(128)(4,1)} %bitcast.6), calls=%async_computation.3 | async-start | bytes 8388608
  1.4 20.8 %slice-start.2 = ((s8[9437184]{0:T(1024)(128)(4,1)}), s8[1048576]{0:T(1024)(128)(4,1)S(1)}, s32[]{:S(2)}) async-start(s8[9437184]{0:T(1024)(128)(4,1)} %bitcast.6), calls=%async_computation.4 | async-start | bytes 2097152
  1.4 20.8 %slice-start.4 = ((s8[9437184]{0:T(1024)(128)(4,1)}), s8[4194304]{0:T(1024)(128)(4,1)S(1)}, s32[]{:S(2)}) async-start(s8[9437184]{0:T(1024)(128)(4,1)} %bitcast.8), calls=%async_computation.6 | async-start | bytes 8388608
  1.4 20.8 %slice-start.5 = ((s8[9437184]{0:T(1024)(128)(4,1)}), s8[1048576]{0:T(1024)(128)(4,1)S(1)}, s32[]{:S(2)}) async-start(s8[9437184]{0:T(1024)(128)(4,1)} %bitcast.8), calls=%async_computation.7 | async-start | bytes 2097152
  1.4 20.8 %copy-start = (bf16[256,256]{1,0:T(8,128)(2,1)S(1)}, bf16[256,256]{1,0:T(8,128)(2,1)}, u32[]{:S(2)}) copy-start(bf16[256,256]{1,0:T(8,128)(2,1)} %constant.5.clone.put_ref) | copy-start | bytes 393220
  1.4 20.8 %copy-start.1 = (bf16[256,256]{1,0:T(8,128)(2,1)S(1)}, bf16[256,256]{1,0:T(8,128)(2,1)}, u32[]{:S(2)}) copy-start(bf16[256,256]{1,0:T(8,128)(2,1)} %constant.4.clone.pick_ref) | copy-start | bytes 393220

commit v5 on v4

--- a/solution.py
+++ b/solution.py
@@ -31,29 +31,39 @@
     return jnp.where(mask, 1.0, 0.0).astype(jnp.bfloat16)
 
 
-def start_kernel(out_ref):
-    out_ref[...] = jnp.zeros_like(out_ref)
-
-
-def send_kernel(
-    per_dev, slot_ref, gate_ref, tokens_ref, cotangent_ref, started, out_ref
-):
-    del started
+def send_kernel(per_dev, *refs):
+    sources, (out_ref, done_ref, *held, sems) = refs[:4], refs[4:]
+    copies = [
+        pltpu.make_async_copy(source, ref, sems.at[i])
+        for i, (source, ref) in enumerate(zip(sources, held))
+    ]
+    for copy in copies:
+        copy.start()
+    slot_ref, gate_ref, tokens_ref, cotangent_ref = held
     shape = (out_ref.shape[0], slot_ref.shape[1])
     device, within = split(lax.broadcasted_iota(jnp.int32, shape, 0), 2 * per_dev)
     kind, place = split(within, per_dev)
+    is_d = kind == 1
+    copies[0].wait()
     match = slot_ref[...] == device * per_dev + place
-    is_d = kind == 1
-    rows = jnp.dot(
-        one_hot(match & ~is_d), tokens_ref[...], preferred_element_type=jnp.float32
-    ) + jnp.dot(
-        one_hot(match & is_d), cotangent_ref[...], preferred_element_type=jnp.float32
-    )
+    pick_x, pick_d = one_hot(match & ~is_d), one_hot(match & is_d)
+    copies[1].wait()
     gate = jnp.sum(jnp.where(match, gate_ref[...], 0.0), axis=1, keepdims=True)
-    out_ref[...] = (rows * jnp.where(is_d[:, :1], gate, 1.0)).astype(out_ref.dtype)
-
-
-def expert_kernel(experts, chunk, recv_ref, w_in_ref, w_out_ref, out_ref):
+    scale = jnp.where(is_d[:, :1], gate, 1.0)
+    copies[2].wait()
+    rows = jnp.dot(pick_x, tokens_ref[...], preferred_element_type=jnp.float32)
+    copies[3].wait()
+    rows += jnp.dot(pick_d, cotangent_ref[...], preferred_element_type=jnp.float32)
+    out_ref[...] = (rows * scale).astype(out_ref.dtype)
+    done_ref[...] = jnp.zeros_like(done_ref)
+
+
+def fetch_kernel(done_ref, out_ref):
+    del done_ref
+    out_ref[...] = jnp.zeros_like(out_ref)
+
+
+def expert_kernel(experts, chunk, _, recv_ref, w_in_ref, w_out_ref, out_ref):
     per_dev = experts * CAP
     total = recv_ref.shape[0]
     devices = total // (2 * per_dev)
@@ -111,7 +121,7 @@
     ).astype(out_ref.dtype)
 
 
-def expert_tiles_kernel(recv_ref, w_in_ref, w_out_ref, pick_ref, put_ref, out_ref):
+def expert_tiles_kernel(_, recv_ref, w_in_ref, w_out_ref, pick_ref, put_ref, out_ref):
     experts, width, hidden = w_in_ref.shape
     per_dev = experts * CAP
     total = recv_ref.shape[0]
@@ -279,7 +289,7 @@
 
 
 VMEM = pl.BlockSpec(memory_space=pltpu.VMEM)
-SHORT = pl.CostEstimate(flops=4_000_000_000, transcendentals=0, bytes_accessed=0)
+ANY = pl.BlockSpec(memory_space=pl.ANY)
 LONG = pl.CostEstimate(flops=20_000_000_000, transcendentals=0, bytes_accessed=0)
 
 
@@ -289,27 +299,33 @@
     per_dev = experts * CAP
     total = devices * per_dev
     slot_row = slot[None, :]
-    started = pl.pallas_call(
-        start_kernel,
-        out_shape=jax.ShapeDtypeStruct((8, 128), jnp.float32),
+    arrays = (slot_row, gate[None, :], tokens, cotangent)
+    arrays = [pltpu.with_memory_space_constraint(a, pltpu.HBM) for a in arrays]
+    mark = jax.ShapeDtypeStruct((8, 128), jnp.float32)
+    send, sent = pl.pallas_call(
+        functools.partial(send_kernel, per_dev),
+        out_shape=(jax.ShapeDtypeStruct((2 * total, width), jnp.bfloat16), mark),
+        in_specs=[ANY] * 4,
+        out_specs=(VMEM, VMEM),
+        scratch_shapes=[pltpu.VMEM(a.shape, a.dtype) for a in arrays]
+        + [pltpu.SemaphoreType.DMA((4,))],
+        compiler_params=pltpu.CompilerParams(vmem_limit_bytes=16 * MIB),
+        name="send",
+    )(*arrays)
+    fetch = pl.pallas_call(
+        fetch_kernel,
+        out_shape=mark,
+        in_specs=[ANY],
         out_specs=VMEM,
         compiler_params=pltpu.CompilerParams(vmem_limit_bytes=MIB),
-        cost_estimate=SHORT,
-        name="start",
-    )()
-    send = pl.pallas_call(
-        functools.partial(send_kernel, per_dev),
-        out_shape=jax.ShapeDtypeStruct((2 * total, width), jnp.bfloat16),
-        in_specs=[VMEM] * 4 + [pl.BlockSpec(memory_space=pl.ANY)],
-        out_specs=VMEM,
-        compiler_params=pltpu.CompilerParams(vmem_limit_bytes=16 * MIB),
         cost_estimate=LONG,
-        name="send",
-    )(slot_row, gate[None, :], tokens, cotangent, started)
+        name="fetch",
+    )(sent)
+    send, fetch = lax.optimization_barrier((send, fetch))
     recv = lax.all_to_all(
         send.reshape(devices, 2 * per_dev, width), AXES, 0, 0, tiled=True
     )
-    operands = (recv.reshape(2 * total, width), w_in, w_out)
+    operands = (fetch, recv.reshape(2 * total, width), w_in, w_out)
     kernel = functools.partial(expert_kernel, experts, 512)
     if tiles_fit(devices, experts, width, hidden):
         operands += tuple(jnp.asarray(m) for m in row_orders(devices, experts))
@@ -317,7 +333,7 @@
     result = pl.pallas_call(
         kernel,
         out_shape=jax.ShapeDtypeStruct((2 * total, width // 2), jnp.bfloat16),
-        in_specs=[VMEM] * len(operands),
+        in_specs=[ANY] + [VMEM] * (len(operands) - 1),
         out_specs=VMEM,
         compiler_params=pltpu.CompilerParams(vmem_limit_bytes=32 * MIB),
         name="expert",
@@ -329,7 +345,7 @@
         functools.partial(token_kernel, per_dev),
         out_shape=jax.ShapeDtypeStruct(tokens.shape, jnp.bfloat16),
         in_specs=[VMEM] * 2,
-        out_specs=pl.BlockSpec(memory_space=pl.ANY),
+        out_specs=ANY,
         scratch_shapes=[
             pltpu.VMEM(tokens.shape, tokens.dtype),
             pltpu.SemaphoreType.DMA((tokens.shape[0] // CHUNK,)),

time: 41.3 us -> 41.6 us (level)
  Pallas kernels: 7.94 us -> 9.54 us
  local copies, waits for them, and re-layouts: 1.39 us -> 0.05 us
    pallas_call x2, Pallas kernels: 0.59 us -> 2.17 us  [the longest x1 2.17 us: per_device(): pl.pallas_call(functools.partial(send_kernel, per_dev), out_shape=(jax.Sh...]
    unnamed x24 -> x18, local copies, waits for them, and re-layouts: 1.39 us -> 0.05 us
where the time goes in v5:
time: 41.6 us; the launch traced here: 41.4 us
  blocking collectives  31.7 us (76%)
  Pallas kernels  9.54 us (23%)
    all_to_all x1, blocking collectives, per_device(): lax.all_to_all(send.reshape(devices, 2 * per_dev, width), AXES, 0, 0, til...  20.2 us
    all_to_all x1, blocking collectives, per_device(): lax.all_to_all(result.reshape(devices, 2 * per_dev, width // 2), AXES, 0,...  11.5 us
    pallas_call x1, Pallas kernels, per_device(): pl.pallas_call(kernel, out_shape=jax.ShapeDtypeStruct((2 * total, width /...  6.17 us
    pallas_call x1, Pallas kernels, per_device(): pl.pallas_call(functools.partial(send_kernel, per_dev), out_shape=(jax.Sh...  2.17 us
    pallas_call x1, Pallas kernels, per_device(): pl.pallas_call(functools.partial(token_kernel, per_dev), out_shape=jax.Sh...  1.21 us

profile of v5, /device:TPU:1, one launch (start us, length us, event | category | flops | bytes accessed | tf_op | source)
XLA Modules:
  0.0 41.4 jit_solution(8781972167927485038)
XLA Ops:
  0.0 0.0 slice-start
  0.0 0.0 slice-start.3
  0.0 2.2 %send.1 = (bf16[256,768]{1,0:T(8,128)(2,1)S(1)}, f32[8,128]{1,0:T(8,128)S(1)}) custom-call(s32[1,512]{1,0:T(1,128)} %bitcast.14, f32[1,512]{1,0:T(1,128)} %bitcast.16, bf16[512,768]{1,0:T(8,128)(2,1)} %refs_2_.1, bf16[512,768]{1,0:T(8,128)(2,1)} %refs_3_.1), custom_call_target="tpu_custom_call" | custom-call | tf_op jit(solution)/shard_map/send/pallas_call | solution.py:305
  2.2 0.0 slice-start.1
  2.2 0.0 slice-start.2
  2.2 0.0 slice-start.4
  2.2 0.0 slice-start.5
  2.2 0.0 copy-start
  2.2 0.0 copy-start.1
  2.3 20.2 %all_to_all.10 = bf16[32,8,768]{2,1,0:T(8,128)(2,1)S(1)} all-to-all(bf16[32,8,768]{2,1,0:T(8,128)(2,1)S(1)} %bitcast.13), channel_id=1, replica_groups=mesh['cross'=4,'island'=8] {'cross','island'}, dimensions={0} | all-to-all | bytes 786432 | tf_op jit(solution)/shard_map/all_to_all | solution.py:325
  22.4 0.0 slice-done
  22.4 0.0 slice-done.3
  22.4 0.0 slice-done.1
  22.5 0.0 slice-done.2
  22.5 0.0 slice-done.4
  22.5 0.0 slice-done.5
  22.5 0.0 copy-done
  22.5 0.0 copy-done.1
  22.5 0.0 copy-start.2
  22.5 6.2 %expert.1 = bf16[256,384]{1,0:T(8,128)(2,1)S(1)} custom-call(f32[8,128]{1,0:T(8,128)S(1)} %fetch.1._, bf16[256,768]{1,0:T(8,128)(2,1)S(1)} %bitcast.10, bf16[2,768,3072]{2,1,0:T(8,128)(2,1)S(1)} %bitcast.7, bf16[2,3072,768]{2,1,0:T(8,128)(2,1)S(1)} %bitcast.9, bf16[256,256]{1,0:T(8,128)(2,1)S(1)} %copy-done.1, bf16[256,256]{1,0:T(8,128)(2,1)S(1)} %copy-done), custom_call_target="tpu_custom_call" | custom-call | tf_op jit(solution)/shard_map/expert/pallas_call | solution.py:333
  28.7 11.5 %all_to_all.11 = bf16[32,8,384]{2,1,0:T(8,128)(2,1)S(1)} all-to-all(bf16[32,8,384]{2,1,0:T(8,128)(2,1)S(1)} %bitcast.11), channel_id=1, replica_groups=mesh['cross'=4,'island'=8] {'cross','island'}, dimensions={0} | all-to-all | bytes 393216 | tf_op jit(solution)/shard_map/all_to_all | solution.py:341
  40.2 0.0 copy-done.2
  40.2 1.2 %token_.1 = bf16[512,768]{1,0:T(8,128)(2,1)} custom-call(s32[1,512]{1,0:T(1,128)S(1)} %bitcast.15, bf16[256,384]{1,0:T(8,128)(2,1)S(1)} %bitcast.12), custom_call_target="tpu_custom_call" | custom-call | tf_op jit(solution)/shard_map/token/pallas_call | solution.py:344
  (3 shorter events, 0.0 us)
Async XLA Ops:
  0.0 22.4 %slice-start = ((s8[9437184]{0:T(1024)(128)(4,1)}), s8[4194304]{0:T(1024)(128)(4,1)S(1)}, s32[]{:S(2)}) async-start(s8[9437184]{0:T(1024)(128)(4,1)} %bitcast.6), calls=%async_computation.2 | async-start | bytes 8388608
  0.0 22.4 %slice-start.3 = ((s8[9437184]{0:T(1024)(128)(4,1)}), s8[4194304]{0:T(1024)(128)(4,1)S(1)}, s32[]{:S(2)}) async-start(s8[9437184]{0:T(1024)(128)(4,1)} %bitcast.8), calls=%async_computation.5 | async-start | bytes 8388608
  2.2 20.3 %slice-start.1 = ((s8[9437184]{0:T(1024)(128)(4,1)}), s8[4194304]{0:T(1024)(128)(4,1)S(1)}, s32[]{:S(2)}) async-start(s8[9437184]{0:T(1024)(128)(4,1)} %bitcast.6), calls=%async_computation.3 | async-start | bytes 8388608
  2.2 20.3 %slice-start.2 = ((s8[9437184]{0:T(1024)(128)(4,1)}), s8[1048576]{0:T(1024)(128)(4,1)S(1)}, s32[]{:S(2)}) async-start(s8[9437184]{0:T(1024)(128)(4,1)} %bitcast.6), calls=%async_computation.4 | async-start | bytes 2097152
  2.2 20.3 %slice-start.4 = ((s8[9437184]{0:T(1024)(128)(4,1)}), s8[4194304]{0:T(1024)(128)(4,1)S(1)}, s32[]{:S(2)}) async-start(s8[9437184]{0:T(1024)(128)(4,1)} %bitcast.8), calls=%async_computation.6 | async-start | bytes 8388608
  2.2 20.3 %slice-start.5 = ((s8[9437184]{0:T(1024)(128)(4,1)}), s8[1048576]{0:T(1024)(128)(4,1)S(1)}, s32[]{:S(2)}) async-start(s8[9437184]{0:T(1024)(128)(4,1)} %bitcast.8), calls=%async_computation.7 | async-start | bytes 2097152
  2.2 20.3 %copy-start = (bf16[256,256]{1,0:T(8,128)(2,1)S(1)}, bf16[256,256]{1,0:T(8,128)(2,1)}, u32[]{:S(2)}) copy-start(bf16[256,256]{1,0:T(8,128)(2,1)} %constant.5.clone.put_ref) | copy-start | bytes 393220
  2.2 20.3 %copy-start.1 = (bf16[256,256]{1,0:T(8,128)(2,1)S(1)}, bf16[256,256]{1,0:T(8,128)(2,1)}, u32[]{:S(2)}) copy-start(bf16[256,256]{1,0:T(8,128)(2,1)} %constant.4.clone.pick_ref) | copy-start | bytes 393220
  22.5 17.7 %copy-start.2 = (s32[512]{0:T(512)S(1)}, s32[512]{0:T(512)}, u32[]{:S(2)}) copy-start(s32[512]{0:T(512)} %param.11) | copy-start | bytes 6148

commit v6 on v4

--- a/solution.py
+++ b/solution.py
@@ -35,22 +35,34 @@
     out_ref[...] = jnp.zeros_like(out_ref)
 
 
-def send_kernel(
-    per_dev, slot_ref, gate_ref, tokens_ref, cotangent_ref, started, out_ref
-):
-    del started
-    shape = (out_ref.shape[0], slot_ref.shape[1])
+def plan_kernel(per_dev, slot_ref, gate_ref, _, x_ref, d_ref, scale_ref, back_ref):
+    shape = x_ref.shape
     device, within = split(lax.broadcasted_iota(jnp.int32, shape, 0), 2 * per_dev)
     kind, place = split(within, per_dev)
     match = slot_ref[...] == device * per_dev + place
     is_d = kind == 1
-    rows = jnp.dot(
-        one_hot(match & ~is_d), tokens_ref[...], preferred_element_type=jnp.float32
-    ) + jnp.dot(
-        one_hot(match & is_d), cotangent_ref[...], preferred_element_type=jnp.float32
-    )
+    x_ref[...] = one_hot(match & ~is_d)
+    d_ref[...] = one_hot(match & is_d)
     gate = jnp.sum(jnp.where(match, gate_ref[...], 0.0), axis=1, keepdims=True)
-    out_ref[...] = (rows * jnp.where(is_d[:, :1], gate, 1.0)).astype(out_ref.dtype)
+    scale = jnp.where(is_d[:, :1], gate, 1.0)
+    scale_ref[...] = jnp.broadcast_to(scale, scale_ref.shape)
+    _, count, total = back_ref.shape
+    device, within = split(
+        lax.broadcasted_iota(jnp.int32, (CHUNK, total), 1), 2 * per_dev
+    )
+    side, place = split(within, per_dev)
+    wanted = device * per_dev + place
+    for c in range(0, count, CHUNK):
+        slot = jnp.broadcast_to(slot_ref[:, c : c + CHUNK], (CHUNK, CHUNK)).T
+        slot = jnp.concatenate([slot] * (total // CHUNK), axis=1)
+        for k in range(2):
+            back_ref[k, c : c + CHUNK] = one_hot((slot == wanted) & (side == k))
+
+
+def send_kernel(x_ref, d_ref, scale_ref, tokens_ref, cotangent_ref, out_ref):
+    rows = jnp.dot(x_ref[...], tokens_ref[...], preferred_element_type=jnp.float32)
+    rows += jnp.dot(d_ref[...], cotangent_ref[...], preferred_element_type=jnp.float32)
+    out_ref[...] = (rows * scale_ref[:, :1]).astype(out_ref.dtype)
 
 
 def expert_kernel(experts, chunk, recv_ref, w_in_ref, w_out_ref, out_ref):
@@ -149,14 +161,13 @@
             ]
             plan = []
             for turn, (e, f) in enumerate(blocks):
-                tiles = [
+                plan += [
                     (kind, turn, e, slice(f, f + TILE), k)
-                    for kind in (PRE, BACK)
+                    for kind in (BACK, PRE)
                     for k in range(depth)
                 ]
                 if turn:
-                    tiles.insert(depth + 1, final)
-                plan += tiles
+                    plan.append(final)
                 final = (FINAL, turn, e, slice(f, f + TILE), 0)
             plans.append(plan + [final])
         last = len(plans[0]) - 1
@@ -170,12 +181,12 @@
             else:
                 pre = pltpu.matmul_pop(acc(unit, PRE, turn))
                 back = pltpu.matmul_pop(acc(unit, BACK, turn))
-                parts = [(back * ramp(pre)).astype(bf16)]
-                if e:
-                    parts.insert(0, jnp.zeros((e * rows, TILE), bf16))
-                parts.append(jnp.zeros((TILE - (e + 1) * rows, TILE), bf16))
-                tile = jnp.concatenate(parts, 0)
-            pltpu.matmul_push_rhs(tile, n % 2, unit, transpose=kind != PRE)
+                parts = [jnp.zeros((rows, TILE), bf16)] * experts
+                parts[e] = (back * ramp(pre)).astype(bf16)
+                tile = jnp.concatenate(parts, 0).T
+                rest = jnp.zeros((TILE, TILE - experts * rows), bf16)
+                tile = jnp.concatenate([tile, rest], 1)
+            pltpu.matmul_push_rhs(tile, n % 2, unit, transpose=kind == BACK)
 
         def multiply(unit, n):
             kind, turn, e, f, k = plans[unit][n]
@@ -252,21 +263,14 @@
     )
 
 
-def token_kernel(per_dev, slot_ref, rows_ref, out_hbm, out_ref, sems):
-    total, half = rows_ref.shape
-    device, within = split(
-        lax.broadcasted_iota(jnp.int32, (CHUNK, total), 1), 2 * per_dev
-    )
-    side, place = split(within, per_dev)
-    wanted = device * per_dev + place
+def token_kernel(back_ref, rows_ref, out_hbm, out_ref, sems):
+    half = rows_ref.shape[1]
     copies = []
-    for c in range(slot_ref.shape[1] // CHUNK):
+    for c in range(out_ref.shape[0] // CHUNK):
         tokens = pl.ds(c * CHUNK, CHUNK)
-        slot = jnp.broadcast_to(slot_ref[:, tokens], (CHUNK, CHUNK)).T
-        slot = jnp.concatenate([slot] * (total // CHUNK), axis=1)
         for k in range(2):
             out_ref[tokens, k * half : (k + 1) * half] = jnp.dot(
-                one_hot((slot == wanted) & (side == k)),
+                back_ref[k, tokens],
                 rows_ref[...],
                 preferred_element_type=jnp.float32,
             ).astype(out_ref.dtype)
@@ -297,15 +301,29 @@
         cost_estimate=SHORT,
         name="start",
     )()
+    picks = jax.ShapeDtypeStruct((2 * total, tokens.shape[0]), jnp.bfloat16)
+    *plan, back = pl.pallas_call(
+        functools.partial(plan_kernel, per_dev),
+        out_shape=(
+            picks,
+            picks,
+            jax.ShapeDtypeStruct((2 * total, 128), jnp.float32),
+            jax.ShapeDtypeStruct((2, tokens.shape[0], 2 * total), jnp.bfloat16),
+        ),
+        in_specs=[VMEM, VMEM, pl.BlockSpec(memory_space=pl.ANY)],
+        out_specs=(VMEM,) * 4,
+        compiler_params=pltpu.CompilerParams(vmem_limit_bytes=16 * MIB),
+        name="plan",
+    )(slot_row, gate[None, :], started)
     send = pl.pallas_call(
-        functools.partial(send_kernel, per_dev),
+        send_kernel,
         out_shape=jax.ShapeDtypeStruct((2 * total, width), jnp.bfloat16),
-        in_specs=[VMEM] * 4 + [pl.BlockSpec(memory_space=pl.ANY)],
+        in_specs=[VMEM] * 5,
         out_specs=VMEM,
         compiler_params=pltpu.CompilerParams(vmem_limit_bytes=16 * MIB),
         cost_estimate=LONG,
         name="send",
-    )(slot_row, gate[None, :], tokens, cotangent, started)
+    )(*plan, tokens, cotangent)
     recv = lax.all_to_all(
         send.reshape(devices, 2 * per_dev, width), AXES, 0, 0, tiled=True
     )
@@ -326,7 +344,7 @@
         result.reshape(devices, 2 * per_dev, width // 2), AXES, 0, 0, tiled=True
     )
     return pl.pallas_call(
-        functools.partial(token_kernel, per_dev),
+        token_kernel,
         out_shape=jax.ShapeDtypeStruct(tokens.shape, jnp.bfloat16),
         in_specs=[VMEM] * 2,
         out_specs=pl.BlockSpec(memory_space=pl.ANY),
@@ -336,7 +354,7 @@
         ],
         compiler_params=pltpu.CompilerParams(vmem_limit_bytes=16 * MIB),
         name="token",
-    )(slot_row, arrived.reshape(2 * total, width // 2))
+    )(back, arrived.reshape(2 * total, width // 2))
 
 
 def solution(mesh):

time: 41.3 us -> 41 us (level)
    pallas_call x2 -> x3, Pallas kernels: 1.8 us -> 1.96 us  [the longest x1 1.14 us: per_device(): pl.pallas_call(token_kernel, out_shape=jax.ShapeDtypeStruct(tokens.shape,...]
where the time goes in v6:
time: 41 us; the launch traced here: 40.9 us
  blocking collectives  31.7 us (77%)
  Pallas kernels  7.91 us (19%)
  local copies, waits for them, and re-layouts  1.15 us (3%)
    all_to_all x1, blocking collectives, per_device(): lax.all_to_all(send.reshape(devices, 2 * per_dev, width), AXES, 0, 0, til...  20.2 us
    all_to_all x1, blocking collectives, per_device(): lax.all_to_all(result.reshape(devices, 2 * per_dev, width // 2), AXES, 0,...  11.5 us
    pallas_call x1, Pallas kernels, per_device(): pl.pallas_call(kernel, out_shape=jax.ShapeDtypeStruct((2 * total, width /...  5.95 us
    unnamed x24, local copies, waits for them, and re-layouts  1.15 us
    pallas_call x1, Pallas kernels, per_device(): pl.pallas_call(token_kernel, out_shape=jax.ShapeDtypeStruct(tokens.shape,...  1.14 us

profile of v6, /device:TPU:1, one launch (start us, length us, event | category | flops | bytes accessed | tf_op | source)
XLA Modules:
  0.0 40.9 jit_solution(5937009650105431151)
XLA Ops:
  0.0 0.0 copy-start.2
  0.0 0.0 copy-start.3
  0.0 0.0 copy-start.5
  0.0 0.0 copy-start.4
  0.0 0.0 slice-start
  0.0 0.0 slice-start.3
  0.1 0.6 %copy-done.2 = s32[512]{0:T(512)S(1)} copy-done((s32[512]{0:T(512)S(1)}, s32[512]{0:T(512)}, u32[]{:S(2)}) %copy-start.2) | copy-done | bytes 2072
  0.7 0.0 copy-done.3
  0.7 0.2 plan.1
  0.9 0.2 copy-done.5
  1.2 0.2 copy-done.4
  1.4 0.0 slice-start.1
  1.4 0.0 slice-start.2
  1.4 0.0 slice-start.4
  1.4 0.0 slice-start.5
  1.4 0.0 copy-start
  1.4 0.0 copy-start.1
  1.4 0.6 %send.1 = bf16[256,768]{1,0:T(8,128)(2,1)S(1)} custom-call(bf16[256,512]{1,0:T(8,128)(2,1)S(1)} %get-tuple-element.10.x_ref, bf16[256,512]{1,0:T(8,128)(2,1)S(1)} %get-tuple-element.11.d_ref, f32[256,128]{1,0:T(8,128)S(1)} %get-tuple-element.12.scale_ref, bf16[512,768]{1,0:T(8,128)(2,1)S(1)} %copy-done.4, bf16[512,768]{1,0:T(8,128)(2,1)S(1)} %copy-done.5), custom_call_target="tpu_custom_call" | custom-call | flops 20000000000 | tf_op jit(solution)/shard_map/send/pallas_call | solution.py:318
  2.0 20.2 %all_to_all.10 = bf16[32,8,768]{2,1,0:T(8,128)(2,1)S(1)} all-to-all(bf16[32,8,768]{2,1,0:T(8,128)(2,1)S(1)} %bitcast.13), channel_id=1, replica_groups=mesh['cross'=4,'island'=8] {'cross','island'}, dimensions={0} | all-to-all | bytes 786432 | tf_op jit(solution)/shard_map/all_to_all | solution.py:327
  22.2 0.0 slice-done
  22.2 0.0 slice-done.3
  22.2 0.0 slice-done.1
  22.2 0.0 slice-done.2
  22.2 0.0 slice-done.4
  22.2 0.0 slice-done.5
  22.2 0.0 copy-done
  22.2 0.0 copy-done.1
  22.3 5.9 %expert.1 = bf16[256,384]{1,0:T(8,128)(2,1)S(1)} custom-call(bf16[256,768]{1,0:T(8,128)(2,1)S(1)} %bitcast.10, bf16[2,768,3072]{2,1,0:T(8,128)(2,1)S(1)} %bitcast.7, bf16[2,3072,768]{2,1,0:T(8,128)(2,1)S(1)} %bitcast.9, bf16[256,256]{1,0:T(8,128)(2,1)S(1)} %copy-done.1, bf16[256,256]{1,0:T(8,128)(2,1)S(1)} %copy-done), custom_call_target="tpu_custom_call" | custom-call | tf_op jit(solution)/shard_map/expert/pallas_call | solution.py:335
  28.2 11.5 %all_to_all.11 = bf16[32,8,384]{2,1,0:T(8,128)(2,1)S(1)} all-to-all(bf16[32,8,384]{2,1,0:T(8,128)(2,1)S(1)} %bitcast.11), channel_id=1, replica_groups=mesh['cross'=4,'island'=8] {'cross','island'}, dimensions={0} | all-to-all | bytes 393216 | tf_op jit(solution)/shard_map/all_to_all | solution.py:343
  39.7 1.1 %token_.1 = bf16[512,768]{1,0:T(8,128)(2,1)} custom-call(bf16[2,512,256]{2,1,0:T(8,128)(2,1)S(1)} %get-tuple-element.9.back_ref, bf16[256,384]{1,0:T(8,128)(2,1)S(1)} %bitcast.12), custom_call_target="tpu_custom_call" | custom-call | tf_op jit(solution)/shard_map/token/pallas_call | solution.py:346
  (3 shorter events, 0.0 us)
Async XLA Ops:
  0.0 0.7 %copy-start.2 = (s32[512]{0:T(512)S(1)}, s32[512]{0:T(512)}, u32[]{:S(2)}) copy-start(s32[512]{0:T(512)} %param.11) | copy-start | bytes 6148
  0.0 0.7 %copy-start.3 = (f32[512]{0:T(512)S(1)}, f32[512]{0:T(512)}, u32[]{:S(2)}) copy-start(f32[512]{0:T(512)} %param.10) | copy-start | bytes 6148
  0.0 1.2 %copy-start.5 = (bf16[512,768]{1,0:T(8,128)(2,1)S(1)}, bf16[512,768]{1,0:T(8,128)(2,1)}, u32[]{:S(2)}) copy-start(bf16[512,768]{1,0:T(8,128)(2,1)} %cotangent_ref.1) | copy-start | bytes 2359300
  0.0 1.4 %copy-start.4 = (bf16[512,768]{1,0:T(8,128)(2,1)S(1)}, bf16[512,768]{1,0:T(8,128)(2,1)}, u32[]{:S(2)}) copy-start(bf16[512,768]{1,0:T(8,128)(2,1)} %tokens_ref.1) | copy-start | bytes 2359300
  0.0 22.2 %slice-start = ((s8[9437184]{0:T(1024)(128)(4,1)}), s8[4194304]{0:T(1024)(128)(4,1)S(1)}, s32[]{:S(2)}) async-start(s8[9437184]{0:T(1024)(128)(4,1)} %bitcast.6), calls=%async_computation.2 | async-start | bytes 8388608
  0.0 22.2 %slice-start.3 = ((s8[9437184]{0:T(1024)(128)(4,1)}), s8[4194304]{0:T(1024)(128)(4,1)S(1)}, s32[]{:S(2)}) async-start(s8[9437184]{0:T(1024)(128)(4,1)} %bitcast.8), calls=%async_computation.5 | async-start | bytes 8388608
  1.4 20.8 %slice-start.1 = ((s8[9437184]{0:T(1024)(128)(4,1)}), s8[4194304]{0:T(1024)(128)(4,1)S(1)}, s32[]{:S(2)}) async-start(s8[9437184]{0:T(1024)(128)(4,1)} %bitcast.6), calls=%async_computation.3 | async-start | bytes 8388608
  1.4 20.8 %slice-start.2 = ((s8[9437184]{0:T(1024)(128)(4,1)}), s8[1048576]{0:T(1024)(128)(4,1)S(1)}, s32[]{:S(2)}) async-start(s8[9437184]{0:T(1024)(128)(4,1)} %bitcast.6), calls=%async_computation.4 | async-start | bytes 2097152
  1.4 20.8 %slice-start.4 = ((s8[9437184]{0:T(1024)(128)(4,1)}), s8[4194304]{0:T(1024)(128)(4,1)S(1)}, s32[]{:S(2)}) async-start(s8[9437184]{0:T(1024)(128)(4,1)} %bitcast.8), calls=%async_computation.6 | async-start | bytes 8388608
  1.4 20.8 %slice-start.5 = ((s8[9437184]{0:T(1024)(128)(4,1)}), s8[1048576]{0:T(1024)(128)(4,1)S(1)}, s32[]{:S(2)}) async-start(s8[9437184]{0:T(1024)(128)(4,1)} %bitcast.8), calls=%async_computation.7 | async-start | bytes 2097152
  1.4 20.8 %copy-start = (bf16[256,256]{1,0:T(8,128)(2,1)S(1)}, bf16[256,256]{1,0:T(8,128)(2,1)}, u32[]{:S(2)}) copy-start(bf16[256,256]{1,0:T(8,128)(2,1)} %constant.5.clone.put_ref) | copy-start | bytes 393220
  1.4 20.8 %copy-start.1 = (bf16[256,256]{1,0:T(8,128)(2,1)S(1)}, bf16[256,256]{1,0:T(8,128)(2,1)}, u32[]{:S(2)}) copy-start(bf16[256,256]{1,0:T(8,128)(2,1)} %constant.4.clone.pick_ref) | copy-start | bytes 393220

commit v7 on v6

--- a/solution.py
+++ b/solution.py
@@ -59,10 +59,16 @@
             back_ref[k, c : c + CHUNK] = one_hot((slot == wanted) & (side == k))
 
 
-def send_kernel(x_ref, d_ref, scale_ref, tokens_ref, cotangent_ref, out_ref):
-    rows = jnp.dot(x_ref[...], tokens_ref[...], preferred_element_type=jnp.float32)
-    rows += jnp.dot(d_ref[...], cotangent_ref[...], preferred_element_type=jnp.float32)
-    out_ref[...] = (rows * scale_ref[:, :1]).astype(out_ref.dtype)
+def tokens_kernel(x_ref, tokens_ref, out_ref):
+    out_ref[...] = jnp.dot(
+        x_ref[...], tokens_ref[...], preferred_element_type=jnp.float32
+    ).astype(out_ref.dtype)
+
+
+def send_kernel(rows_ref, d_ref, scale_ref, cotangent_ref, out_ref):
+    rows = jnp.dot(d_ref[...], cotangent_ref[...], preferred_element_type=jnp.float32)
+    rows = rows * scale_ref[:, :1] + rows_ref[...].astype(jnp.float32)
+    out_ref[...] = rows.astype(out_ref.dtype)
 
 
 def expert_kernel(experts, chunk, recv_ref, w_in_ref, w_out_ref, out_ref):
@@ -315,15 +321,25 @@
         compiler_params=pltpu.CompilerParams(vmem_limit_bytes=16 * MIB),
         name="plan",
     )(slot_row, gate[None, :], started)
+    pick_x, pick_d, scale = plan
+    rows = jax.ShapeDtypeStruct((2 * total, width), jnp.bfloat16)
+    placed = pl.pallas_call(
+        tokens_kernel,
+        out_shape=rows,
+        in_specs=[VMEM] * 2,
+        out_specs=VMEM,
+        compiler_params=pltpu.CompilerParams(vmem_limit_bytes=16 * MIB),
+        name="tokens",
+    )(pick_x, tokens)
     send = pl.pallas_call(
         send_kernel,
-        out_shape=jax.ShapeDtypeStruct((2 * total, width), jnp.bfloat16),
-        in_specs=[VMEM] * 5,
+        out_shape=rows,
+        in_specs=[VMEM] * 4,
         out_specs=VMEM,
         compiler_params=pltpu.CompilerParams(vmem_limit_bytes=16 * MIB),
         cost_estimate=LONG,
         name="send",
-    )(*plan, tokens, cotangent)
+    )(placed, pick_d, scale, cotangent)
     recv = lax.all_to_all(
         send.reshape(devices, 2 * per_dev, width), AXES, 0, 0, tiled=True
     )

time: 41 us -> 41 us (level)
  no operation moved by 1% of the time
where the time goes in v7:
time: 41 us; the launch traced here: 40.9 us
  blocking collectives  31.7 us (77%)
  Pallas kernels  8.07 us (20%)
  local copies, waits for them, and re-layouts  0.94 us (2%)
    all_to_all x1, blocking collectives, per_device(): lax.all_to_all(send.reshape(devices, 2 * per_dev, width), AXES, 0, 0, til...  20.2 us
    all_to_all x1, blocking collectives, per_device(): lax.all_to_all(result.reshape(devices, 2 * per_dev, width // 2), AXES, 0,...  11.5 us
    pallas_call x1, Pallas kernels, per_device(): pl.pallas_call(kernel, out_shape=jax.ShapeDtypeStruct((2 * total, width /...  5.94 us
    pallas_call x1, Pallas kernels, per_device(): pl.pallas_call(token_kernel, out_shape=jax.ShapeDtypeStruct(tokens.shape,...  1.14 us
    unnamed x24, local copies, waits for them, and re-layouts  0.94 us

profile of v7, /device:TPU:1, one launch (start us, length us, event | category | flops | bytes accessed | tf_op | source)
XLA Modules:
  0.0 40.9 jit_solution(14427472468605433623)
XLA Ops:
  0.0 0.0 copy-start.3
  0.0 0.0 copy-start.4
  0.0 0.0 copy-start
  0.0 0.0 copy-start.5
  0.0 0.7 %copy-done.3 = s32[512]{0:T(512)S(1)} copy-done((s32[512]{0:T(512)S(1)}, s32[512]{0:T(512)}, u32[]{:S(2)}) %copy-start.3) | copy-done | bytes 2072
  0.7 0.0 copy-done.4
  0.7 0.2 plan.1
  0.9 0.2 copy-done
  1.2 0.0 slice-start
  1.2 0.0 slice-start.3
  1.2 0.4 tokens.1.rows_ref
  1.5 0.0 copy-done.5
  1.6 0.0 slice-start.1
  1.6 0.0 slice-start.2
  1.6 0.0 slice-start.4
  1.6 0.0 slice-start.5
  1.6 0.0 copy-start.1
  1.6 0.0 copy-start.2
  1.6 0.4 send.1
  2.0 20.2 %all_to_all.10 = bf16[32,8,768]{2,1,0:T(8,128)(2,1)S(1)} all-to-all(bf16[32,8,768]{2,1,0:T(8,128)(2,1)S(1)} %bitcast.13), channel_id=1, replica_groups=mesh['cross'=4,'island'=8] {'cross','island'}, dimensions={0} | all-to-all | bytes 786432 | tf_op jit(solution)/shard_map/all_to_all | solution.py:343
  22.2 0.0 slice-done
  22.2 0.0 slice-done.3
  22.2 0.0 slice-done.1
  22.2 0.0 slice-done.2
  22.2 0.0 slice-done.4
  22.2 0.0 slice-done.5
  22.2 0.0 copy-done.1
  22.2 0.0 copy-done.2
  22.3 5.9 %expert.1 = bf16[256,384]{1,0:T(8,128)(2,1)S(1)} custom-call(bf16[256,768]{1,0:T(8,128)(2,1)S(1)} %bitcast.10, bf16[2,768,3072]{2,1,0:T(8,128)(2,1)S(1)} %bitcast.7, bf16[2,3072,768]{2,1,0:T(8,128)(2,1)S(1)} %bitcast.9, bf16[256,256]{1,0:T(8,128)(2,1)S(1)} %copy-done.2, bf16[256,256]{1,0:T(8,128)(2,1)S(1)} %copy-done.1), custom_call_target="tpu_custom_call" | custom-call | tf_op jit(solution)/shard_map/expert/pallas_call | solution.py:351
  28.2 11.5 %all_to_all.11 = bf16[32,8,384]{2,1,0:T(8,128)(2,1)S(1)} all-to-all(bf16[32,8,384]{2,1,0:T(8,128)(2,1)S(1)} %bitcast.11), channel_id=1, replica_groups=mesh['cross'=4,'island'=8] {'cross','island'}, dimensions={0} | all-to-all | bytes 393216 | tf_op jit(solution)/shard_map/all_to_all | solution.py:359
  39.7 1.1 %token_.1 = bf16[512,768]{1,0:T(8,128)(2,1)} custom-call(bf16[2,512,256]{2,1,0:T(8,128)(2,1)S(1)} %get-tuple-element.9.back_ref, bf16[256,384]{1,0:T(8,128)(2,1)S(1)} %bitcast.12), custom_call_target="tpu_custom_call" | custom-call | tf_op jit(solution)/shard_map/token/pallas_call | solution.py:362
  (3 shorter events, 0.0 us)
Async XLA Ops:
  0.0 0.7 %copy-start.3 = (s32[512]{0:T(512)S(1)}, s32[512]{0:T(512)}, u32[]{:S(2)}) copy-start(s32[512]{0:T(512)} %param.11) | copy-start | bytes 6148
  0.0 0.7 %copy-start.4 = (f32[512]{0:T(512)S(1)}, f32[512]{0:T(512)}, u32[]{:S(2)}) copy-start(f32[512]{0:T(512)} %param.10) | copy-start | bytes 6148
  0.0 1.2 %copy-start = (bf16[512,768]{1,0:T(8,128)(2,1)S(1)}, bf16[512,768]{1,0:T(8,128)(2,1)}, u32[]{:S(2)}) copy-start(bf16[512,768]{1,0:T(8,128)(2,1)} %tokens_ref.1) | copy-start | bytes 2359300
  0.0 1.5 %copy-start.5 = (bf16[512,768]{1,0:T(8,128)(2,1)S(1)}, bf16[512,768]{1,0:T(8,128)(2,1)}, u32[]{:S(2)}) copy-start(bf16[512,768]{1,0:T(8,128)(2,1)} %cotangent_ref.1) | copy-start | bytes 2359300
  1.2 21.0 %slice-start = ((s8[9437184]{0:T(1024)(128)(4,1)}), s8[4194304]{0:T(1024)(128)(4,1)S(1)}, s32[]{:S(2)}) async-start(s8[9437184]{0:T(1024)(128)(4,1)} %bitcast.6), calls=%async_computation.2 | async-start | bytes 8388608
  1.2 21.0 %slice-start.3 = ((s8[9437184]{0:T(1024)(128)(4,1)}), s8[4194304]{0:T(1024)(128)(4,1)S(1)}, s32[]{:S(2)}) async-start(s8[9437184]{0:T(1024)(128)(4,1)} %bitcast.8), calls=%async_computation.5 | async-start | bytes 8388608
  1.6 20.6 %slice-start.1 = ((s8[9437184]{0:T(1024)(128)(4,1)}), s8[4194304]{0:T(1024)(128)(4,1)S(1)}, s32[]{:S(2)}) async-start(s8[9437184]{0:T(1024)(128)(4,1)} %bitcast.6), calls=%async_computation.3 | async-start | bytes 8388608
  1.6 20.6 %slice-start.2 = ((s8[9437184]{0:T(1024)(128)(4,1)}), s8[1048576]{0:T(1024)(128)(4,1)S(1)}, s32[]{:S(2)}) async-start(s8[9437184]{0:T(1024)(128)(4,1)} %bitcast.6), calls=%async_computation.4 | async-start | bytes 2097152
  1.6 20.6 %slice-start.4 = ((s8[9437184]{0:T(1024)(128)(4,1)}), s8[4194304]{0:T(1024)(128)(4,1)S(1)}, s32[]{:S(2)}) async-start(s8[9437184]{0:T(1024)(128)(4,1)} %bitcast.8), calls=%async_computation.6 | async-start | bytes 8388608
  1.6 20.6 %slice-start.5 = ((s8[9437184]{0:T(1024)(128)(4,1)}), s8[1048576]{0:T(1024)(128)(4,1)S(1)}, s32[]{:S(2)}) async-start(s8[9437184]{0:T(1024)(128)(4,1)} %bitcast.8), calls=%async_computation.7 | async-start | bytes 2097152
  1.6 20.6 %copy-start.1 = (bf16[256,256]{1,0:T(8,128)(2,1)S(1)}, bf16[256,256]{1,0:T(8,128)(2,1)}, u32[]{:S(2)}) copy-start(bf16[256,256]{1,0:T(8,128)(2,1)} %constant.5.clone.put_ref) | copy-start | bytes 393220
  1.6 20.6 %copy-start.2 = (bf16[256,256]{1,0:T(8,128)(2,1)S(1)}, bf16[256,256]{1,0:T(8,128)(2,1)}, u32[]{:S(2)}) copy-start(bf16[256,256]{1,0:T(8,128)(2,1)} %constant.4.clone.pick_ref) | copy-start | bytes 393220

commit v8 on v6

--- a/solution.py
+++ b/solution.py
@@ -14,6 +14,7 @@
 TILE = 256
 UNITS = 2
 CHUNK = 128
+LEAVE = 256
 PRE, BACK, FINAL = range(3)
 
 
@@ -266,8 +267,8 @@
 def token_kernel(back_ref, rows_ref, out_hbm, out_ref, sems):
     half = rows_ref.shape[1]
     copies = []
-    for c in range(out_ref.shape[0] // CHUNK):
-        tokens = pl.ds(c * CHUNK, CHUNK)
+    for c in range(out_ref.shape[0] // LEAVE):
+        tokens = pl.ds(c * LEAVE, LEAVE)
         for k in range(2):
             out_ref[tokens, k * half : (k + 1) * half] = jnp.dot(
                 back_ref[k, tokens],
@@ -350,7 +351,7 @@
         out_specs=pl.BlockSpec(memory_space=pl.ANY),
         scratch_shapes=[
             pltpu.VMEM(tokens.shape, tokens.dtype),
-            pltpu.SemaphoreType.DMA((tokens.shape[0] // CHUNK,)),
+            pltpu.SemaphoreType.DMA((tokens.shape[0] // LEAVE,)),
         ],
         compiler_params=pltpu.CompilerParams(vmem_limit_bytes=16 * MIB),
         name="token",

time: 41 us -> 41.1 us (level)
  no operation moved by 1% of the time
where the time goes in v8:
time: 41.1 us; the launch traced here: 40.9 us
  blocking collectives  31.7 us (77%)
  Pallas kernels  7.96 us (19%)
  local copies, waits for them, and re-layouts  1.15 us (3%)
    all_to_all x1, blocking collectives, per_device(): lax.all_to_all(send.reshape(devices, 2 * per_dev, width), AXES, 0, 0, til...  20.2 us
    all_to_all x1, blocking collectives, per_device(): lax.all_to_all(result.reshape(devices, 2 * per_dev, width // 2), AXES, 0,...  11.5 us
    pallas_call x1, Pallas kernels, per_device(): pl.pallas_call(kernel, out_shape=jax.ShapeDtypeStruct((2 * total, width /...  5.95 us
    pallas_call x1, Pallas kernels, per_device(): pl.pallas_call(token_kernel, out_shape=jax.ShapeDtypeStruct(tokens.shape,...  1.19 us
    unnamed x24, local copies, waits for them, and re-layouts  1.15 us

profile of v8, /device:TPU:1, one launch (start us, length us, event | category | flops | bytes accessed | tf_op | source)
XLA Modules:
  0.0 40.9 jit_solution(5190841448761106747)
XLA Ops:
  0.0 0.0 copy-start.2
  0.0 0.0 copy-start.3
  0.0 0.0 copy-start.5
  0.0 0.0 copy-start.4
  0.0 0.0 slice-start
  0.0 0.0 slice-start.3
  0.1 0.6 %copy-done.2 = s32[512]{0:T(512)S(1)} copy-done((s32[512]{0:T(512)S(1)}, s32[512]{0:T(512)}, u32[]{:S(2)}) %copy-start.2) | copy-done | bytes 2072
  0.7 0.0 copy-done.3
  0.7 0.2 plan.1
  0.9 0.2 copy-done.5
  1.2 0.2 copy-done.4
  1.4 0.0 slice-start.1
  1.4 0.0 slice-start.2
  1.4 0.0 slice-start.4
  1.4 0.0 slice-start.5
  1.4 0.0 copy-start
  1.4 0.0 copy-start.1
  1.4 0.6 %send.1 = bf16[256,768]{1,0:T(8,128)(2,1)S(1)} custom-call(bf16[256,512]{1,0:T(8,128)(2,1)S(1)} %get-tuple-element.10.x_ref, bf16[256,512]{1,0:T(8,128)(2,1)S(1)} %get-tuple-element.11.d_ref, f32[256,128]{1,0:T(8,128)S(1)} %get-tuple-element.12.scale_ref, bf16[512,768]{1,0:T(8,128)(2,1)S(1)} %copy-done.4, bf16[512,768]{1,0:T(8,128)(2,1)S(1)} %copy-done.5), custom_call_target="tpu_custom_call" | custom-call | flops 20000000000 | tf_op jit(solution)/shard_map/send/pallas_call | solution.py:319
  2.0 20.2 %all_to_all.10 = bf16[32,8,768]{2,1,0:T(8,128)(2,1)S(1)} all-to-all(bf16[32,8,768]{2,1,0:T(8,128)(2,1)S(1)} %bitcast.13), channel_id=1, replica_groups=mesh['cross'=4,'island'=8] {'cross','island'}, dimensions={0} | all-to-all | bytes 786432 | tf_op jit(solution)/shard_map/all_to_all | solution.py:328
  22.2 0.0 slice-done
  22.2 0.0 slice-done.3
  22.2 0.0 slice-done.1
  22.2 0.0 slice-done.2
  22.2 0.0 slice-done.4
  22.2 0.0 slice-done.5
  22.2 0.0 copy-done
  22.2 0.0 copy-done.1
  22.3 5.9 %expert.1 = bf16[256,384]{1,0:T(8,128)(2,1)S(1)} custom-call(bf16[256,768]{1,0:T(8,128)(2,1)S(1)} %bitcast.10, bf16[2,768,3072]{2,1,0:T(8,128)(2,1)S(1)} %bitcast.7, bf16[2,3072,768]{2,1,0:T(8,128)(2,1)S(1)} %bitcast.9, bf16[256,256]{1,0:T(8,128)(2,1)S(1)} %copy-done.1, bf16[256,256]{1,0:T(8,128)(2,1)S(1)} %copy-done), custom_call_target="tpu_custom_call" | custom-call | tf_op jit(solution)/shard_map/expert/pallas_call | solution.py:336
  28.2 11.5 %all_to_all.11 = bf16[32,8,384]{2,1,0:T(8,128)(2,1)S(1)} all-to-all(bf16[32,8,384]{2,1,0:T(8,128)(2,1)S(1)} %bitcast.11), channel_id=1, replica_groups=mesh['cross'=4,'island'=8] {'cross','island'}, dimensions={0} | all-to-all | bytes 393216 | tf_op jit(solution)/shard_map/all_to_all | solution.py:344
  39.7 1.2 %token_.1 = bf16[512,768]{1,0:T(8,128)(2,1)} custom-call(bf16[2,512,256]{2,1,0:T(8,128)(2,1)S(1)} %get-tuple-element.9.back_ref, bf16[256,384]{1,0:T(8,128)(2,1)S(1)} %bitcast.12), custom_call_target="tpu_custom_call" | custom-call | tf_op jit(solution)/shard_map/token/pallas_call | solution.py:347
  (3 shorter events, 0.0 us)
Async XLA Ops:
  0.0 0.7 %copy-start.2 = (s32[512]{0:T(512)S(1)}, s32[512]{0:T(512)}, u32[]{:S(2)}) copy-start(s32[512]{0:T(512)} %param.11) | copy-start | bytes 6148
  0.0 0.7 %copy-start.3 = (f32[512]{0:T(512)S(1)}, f32[512]{0:T(512)}, u32[]{:S(2)}) copy-start(f32[512]{0:T(512)} %param.10) | copy-start | bytes 6148
  0.0 1.2 %copy-start.5 = (bf16[512,768]{1,0:T(8,128)(2,1)S(1)}, bf16[512,768]{1,0:T(8,128)(2,1)}, u32[]{:S(2)}) copy-start(bf16[512,768]{1,0:T(8,128)(2,1)} %cotangent_ref.1) | copy-start | bytes 2359300
  0.0 1.4 %copy-start.4 = (bf16[512,768]{1,0:T(8,128)(2,1)S(1)}, bf16[512,768]{1,0:T(8,128)(2,1)}, u32[]{:S(2)}) copy-start(bf16[512,768]{1,0:T(8,128)(2,1)} %tokens_ref.1) | copy-start | bytes 2359300
  0.0 22.2 %slice-start = ((s8[9437184]{0:T(1024)(128)(4,1)}), s8[4194304]{0:T(1024)(128)(4,1)S(1)}, s32[]{:S(2)}) async-start(s8[9437184]{0:T(1024)(128)(4,1)} %bitcast.6), calls=%async_computation.2 | async-start | bytes 8388608
  0.0 22.2 %slice-start.3 = ((s8[9437184]{0:T(1024)(128)(4,1)}), s8[4194304]{0:T(1024)(128)(4,1)S(1)}, s32[]{:S(2)}) async-start(s8[9437184]{0:T(1024)(128)(4,1)} %bitcast.8), calls=%async_computation.5 | async-start | bytes 8388608
  1.4 20.8 %slice-start.1 = ((s8[9437184]{0:T(1024)(128)(4,1)}), s8[4194304]{0:T(1024)(128)(4,1)S(1)}, s32[]{:S(2)}) async-start(s8[9437184]{0:T(1024)(128)(4,1)} %bitcast.6), calls=%async_computation.3 | async-start | bytes 8388608
  1.4 20.8 %slice-start.2 = ((s8[9437184]{0:T(1024)(128)(4,1)}), s8[1048576]{0:T(1024)(128)(4,1)S(1)}, s32[]{:S(2)}) async-start(s8[9437184]{0:T(1024)(128)(4,1)} %bitcast.6), calls=%async_computation.4 | async-start | bytes 2097152
  1.4 20.8 %slice-start.4 = ((s8[9437184]{0:T(1024)(128)(4,1)}), s8[4194304]{0:T(1024)(128)(4,1)S(1)}, s32[]{:S(2)}) async-start(s8[9437184]{0:T(1024)(128)(4,1)} %bitcast.8), calls=%async_computation.6 | async-start | bytes 8388608
  1.4 20.8 %slice-start.5 = ((s8[9437184]{0:T(1024)(128)(4,1)}), s8[1048576]{0:T(1024)(128)(4,1)S(1)}, s32[]{:S(2)}) async-start(s8[9437184]{0:T(1024)(128)(4,1)} %bitcast.8), calls=%async_computation.7 | async-start | bytes 2097152
  1.4 20.8 %copy-start = (bf16[256,256]{1,0:T(8,128)(2,1)S(1)}, bf16[256,256]{1,0:T(8,128)(2,1)}, u32[]{:S(2)}) copy-start(bf16[256,256]{1,0:T(8,128)(2,1)} %constant.5.clone.put_ref) | copy-start | bytes 393220
  1.4 20.8 %copy-start.1 = (bf16[256,256]{1,0:T(8,128)(2,1)S(1)}, bf16[256,256]{1,0:T(8,128)(2,1)}, u32[]{:S(2)}) copy-start(bf16[256,256]{1,0:T(8,128)(2,1)} %constant.4.clone.pick_ref) | copy-start | bytes 393220
